TPU v7x, 32 devices: a whole 2x2x4 slice. The times are simulated.
32 devices in a mesh: expert: 8 (over y, x, core), dp: 4 (over z).
Axes of the slice: x: 2, y: 2, z: 4, core: 2. Of those that a mesh axis runs over, the one named last changes fastest.
Arguments:
- tokens: bfloat16 [4096, 2048], P(('expert', 'dp')), may hold values from -6 to 6
- cotangent: bfloat16 [4096, 2048], P(('expert', 'dp')), may hold values from -6 to 6
- expert_ids: int32 [4096, 8], P(('expert', 'dp')), may hold values from 0 to 31, all different within a row; in each aligned block of 128 rows (0 to 127, 128 to 255, ...) at most 40 rows name the same one
- combine_weights: float32 [4096, 8], P(('expert', 'dp')), may hold values from 0.1 to 1
- w_gate: bfloat16 [32, 2048, 384], P('expert'), may hold values from -0.125 to 0.125
- w_up: bfloat16 [32, 2048, 384], P('expert'), may hold values from -0.125 to 0.125
- w_down: bfloat16 [32, 2048, 384], P('expert'), may hold values from -0.3125 to 0.3125
- swap_flags: int32 [4], replicated, may hold values 0 or 1
Outputs:
- mixed: bfloat16 [4096, 2048], P(('expert', 'dp'))
- input_grad: bfloat16 [4096, 2048], P(('expert', 'dp'))
- grad_gate: bfloat16 [32, 2048, 384], P('expert', 'dp')
- grad_up: bfloat16 [32, 2048, 384], P('expert', 'dp')
- grad_down: bfloat16 [32, 2048, 384], P('expert', 'dp')
Inputs may be any that keep to these rules, and one draw needn't show every extreme that they name: `expert_ids`: in each aligned block of 128 token rows (the rows of one device) no expert is named by more than 40 rows, a bound that some block reaches. `swap_flags`: entry j concerns the pair of expert-axis indices j and j + 4.
All inputs are finite; a program needn't handle non-finite values.
Results may differ from a plain program's by a relative error of at most 0.0095.
Values may be sent and summed in bfloat16 or wider, within the bound.
A program may use at most 192 MiB of HBM per device.

v0:
```python
import jax
import jax.numpy as jnp
from jax import lax
from jax.sharding import PartitionSpec as P


def partner(value, axis, bit):
    mask = 2**bit
    pairs = [(source, source ^ mask) for source in range(lax.axis_size(axis))]
    return lax.ppermute(value, axis, pairs)


def flag_lookup(flags, devices, half):
    matches = (devices % half)[..., None] == jnp.arange(half, dtype=jnp.int32)
    return jnp.sum(jnp.where(matches, flags, 0), axis=-1) == 1


def replace_last(whole, own_last, peer_last, flag_here):
    chosen = jnp.where(flag_here, peer_last, own_last)
    return jnp.concatenate([whole[: whole.shape[0] - 1], chosen[None]], axis=0)


def expert_forward(received, gate_now, up_now, down_now):
    gate_pre = jnp.einsum("nscd,sdf->nscf", received, gate_now, preferred_element_type=jnp.float32)
    up_pre = jnp.einsum("nscd,sdf->nscf", received, up_now, preferred_element_type=jnp.float32)
    sigma = jax.nn.sigmoid(gate_pre)
    hidden = (gate_pre * sigma * up_pre).astype(jnp.bfloat16)
    expert_out = jnp.einsum(
        "nscf,sdf->nscd", hidden, down_now, preferred_element_type=jnp.float32
    ).astype(jnp.bfloat16)
    return (gate_pre, up_pre, sigma, hidden, expert_out)


def expert_backward(cot_recv, gate_pre, up_pre, sigma, gate_now, up_now, down_now):
    hidden_cot = jnp.einsum(
        "nscd,sdf->nscf", cot_recv, down_now, preferred_element_type=jnp.float32
    )
    gate_cot = (hidden_cot * up_pre * sigma * (1.0 + gate_pre * (1.0 - sigma))).astype(jnp.bfloat16)
    up_cot = (hidden_cot * gate_pre * sigma).astype(jnp.bfloat16)
    input_terms = (
        jnp.einsum("nscf,sdf->nscd", gate_cot, gate_now, preferred_element_type=jnp.float32)
        + jnp.einsum("nscf,sdf->nscd", up_cot, up_now, preferred_element_type=jnp.float32)
    ).astype(jnp.bfloat16)
    return (gate_cot, up_cot, input_terms)


def local(tokens, cotangent, expert_ids, combine_weights, w_gate, w_up, w_down, swap_flags):
    tok_rows, width = tokens.shape
    top_count = expert_ids.shape[1]
    per_device = w_gate.shape[0]
    groups = lax.axis_size("expert")
    half = groups // 2
    pair_bit = groups.bit_length() - 2
    experts_all = groups * per_device
    capacity = tok_rows * top_count * 5 // (4 * experts_all)
    route_count = tok_rows * top_count
    flag_here = flag_lookup(swap_flags, lax.axis_index("expert"), half)
    route_expert = expert_ids.reshape(route_count)
    home_device = route_expert // per_device
    slot_index = route_expert % per_device
    moved = flag_lookup(swap_flags, home_device, half) & (slot_index == per_device - 1)
    owner = jnp.where(moved, (home_device + half) % groups, home_device)
    own_last = (w_gate[per_device - 1], w_up[per_device - 1], w_down[per_device - 1])
    peer_last = partner(
        (w_gate[per_device - 1], w_up[per_device - 1], w_down[per_device - 1]), "expert", pair_bit
    )
    gate_now = replace_last(w_gate, own_last[0], peer_last[0], flag_here)
    up_now = replace_last(w_up, own_last[1], peer_last[1], flag_here)
    down_now = replace_last(w_down, own_last[2], peer_last[2], flag_here)
    one_hot = (route_expert[:, None] == jnp.arange(experts_all, dtype=jnp.int32)[None, :]).astype(
        jnp.int32
    )
    rank_in = jnp.sum(jnp.cumsum(one_hot, axis=0) * one_hot, axis=1) - 1
    target = (owner * per_device + slot_index) * capacity + rank_in
    buffer_rows = experts_all * capacity
    source_route = (
        jnp.full((buffer_rows,), -1, jnp.int32)
        .at[target]
        .set(jnp.arange(route_count, dtype=jnp.int32))
    )
    filled = (source_route >= 0)[:, None]
    safe_route = jnp.maximum(source_route, 0)
    layout = (groups, per_device, capacity, width)
    zero_bf = jnp.zeros((), jnp.bfloat16)
    send_rows = jnp.where(filled, tokens[safe_route // top_count], zero_bf).reshape(layout)
    route_cot = (combine_weights[:, :, None] * cotangent[:, None, :].astype(jnp.float32)).astype(
        jnp.bfloat16
    )
    route_cot = route_cot.reshape(route_count, width)
    send_cot = jnp.where(filled, route_cot[safe_route], zero_bf).reshape(layout)
    received = lax.all_to_all(send_rows, "expert", split_axis=0, concat_axis=0, tiled=True)
    gate_pre, up_pre, sigma, hidden, expert_out = expert_forward(
        received, gate_now, up_now, down_now
    )
    returned = lax.all_to_all(expert_out, "expert", split_axis=0, concat_axis=0, tiled=True)
    cot_recv = lax.all_to_all(send_cot, "expert", split_axis=0, concat_axis=0, tiled=True)
    gate_cot, up_cot, input_terms = expert_backward(
        cot_recv, gate_pre, up_pre, sigma, gate_now, up_now, down_now
    )
    input_back = lax.all_to_all(input_terms, "expert", split_axis=0, concat_axis=0, tiled=True)
    route_out = returned.reshape(buffer_rows, width)[target].reshape(tok_rows, top_count, width)
    mixed = jnp.sum(combine_weights[:, :, None] * route_out.astype(jnp.float32), axis=1).astype(
        jnp.bfloat16
    )
    route_grad = input_back.reshape(buffer_rows, width)[target].reshape(tok_rows, top_count, width)
    input_grad = jnp.sum(route_grad.astype(jnp.float32), axis=1).astype(jnp.bfloat16)
    partials = (
        jnp.einsum("nscd,nscf->sdf", received, gate_cot, preferred_element_type=jnp.float32),
        jnp.einsum("nscd,nscf->sdf", received, up_cot, preferred_element_type=jnp.float32),
        jnp.einsum("nscd,nscf->sdf", cot_recv, hidden, preferred_element_type=jnp.float32),
    )
    summed = (
        lax.psum_scatter(
            partials[0].astype(jnp.bfloat16), "dp", scatter_dimension=1, tiled=True
        ).astype(jnp.float32),
        lax.psum_scatter(
            partials[1].astype(jnp.bfloat16), "dp", scatter_dimension=1, tiled=True
        ).astype(jnp.float32),
        lax.psum_scatter(
            partials[2].astype(jnp.bfloat16), "dp", scatter_dimension=1, tiled=True
        ).astype(jnp.float32),
    )
    grad_gate = summed[0].astype(jnp.bfloat16)
    grad_up = summed[1].astype(jnp.bfloat16)
    grad_down = summed[2].astype(jnp.bfloat16)
    return (mixed, input_grad, grad_gate, grad_up, grad_down)


def solution(mesh):
    return jax.shard_map(
        local,
        mesh=mesh,
        in_specs=(
            P(("expert", "dp"), None),
            P(("expert", "dp"), None),
            P(("expert", "dp"), None),
            P(("expert", "dp"), None),
            P("expert", None, None),
            P("expert", None, None),
            P("expert", None, None),
            P(),
        ),
        out_specs=(
            P(("expert", "dp"), None),
            P(("expert", "dp"), None),
            P("expert", "dp", None),
            P("expert", "dp", None),
            P("expert", "dp", None),
        ),
        check_vma=False,
    )
```

profile of v0, /device:TPU:0, one launch (start us, length us, event | category | flops | bytes accessed | tf_op | source)
XLA Modules:
  0.0 662.0 jit_solution(16506030833322742898)
XLA Ops:
  7.2 0.8 copy.42
  8.0 0.1 eq.89
  8.1 0.1 reshape.264
  8.2 0.1 reshape.265
  8.3 9.0 %reduce-window.6 = s32[32,8,128]{2,1,0:T(8,128)S(1)} reduce-window(s32[32,8,128]{2,1,0:T(8,128)S(1)} %fusion.26, s32[]{:T(128)} %constant.82.clone.1), window={size=1x1x128 pad=0_0x0_0x127_0}, to_apply=%region_2.3 | reduce-window | flops 4161536 | bytes 262148 | tf_op jit(solution)/shard_map/reduce-window
  17.3 0.1 slice.43
  17.4 0.1 copy.45
  17.6 0.1 copy.46
  17.7 0.1 broadcast_add_fusion
  17.9 0.7 select_reduce_fusion
  18.6 0.1 compare_select_fusion
  18.7 4.3 scatter_custom_fusion
  23.1 1.1 convert_element_type.67
  24.2 0.8 copy.41
  25.0 0.1 mul.84
  25.1 0.1 broadcast_in_dim.65
  25.2 2.5 fusion.1
  27.7 13.6 %gather_fusion.2 = bf16[1280,2048]{1,0:T(8,128)(2,1)} fusion(bf16[1024,2048]{1,0:T(8,128)(2,1)} %fusion.1, s32[2048]{0:T(1024)S(1)} %get-tuple-element.12), kind=kCustom, calls=%fused_computation.2 | custom fusion | bytes 10490880 | tf_op jit(solution)/shard_map/gather | solution.py:90
  41.3 6.2 gather_fusion
  47.4 8.7 %broadcast_select_fusion = (bf16[8,4,40,2048]{3,2,1,0:T(8,128)(2,1)}, bf16[8,4,40,2048]{3,2,1,0:T(8,128)(2,1)}) fusion(bf16[8,4,40,2048]{3,2,1,0:T(8,128)(2,1)} %bitcast.126, pred[8,4,40]{2,1,0:T(4,128)(4,1)S(1)} %broadcast_in_dim.65, bf16[8,4,40,2048]{3,2,1,0:T(8,128)(2,1)} %bitcast.127), kind=kLoop, calls=%fused_computation.20 | loop fusion | flops 5242880 | bytes 20972800 | tf_op jit(solution)/shard_map/jit(_where)/select_n | solution.py:90
  56.2 5.2 all-to-all-start
  61.3 2.7 slice_bitcast_fusion
  64.0 2.4 collective-permute-start.2
  66.4 55.5 %all-to-all-done = bf16[8,4,40,2048]{3,2,1,0:T(8,128)(2,1)} async-done(((bf16[8,4,40,2048]{3,2,1,0:T(8,128)(2,1)}), bf16[8,4,40,2048]{3,2,1,0:T(8,128)(2,1)}, u32[]{:S(2)}, u32[]{:S(2)}) %all-to-all-start) | async-done | bytes 5242912 | tf_op jit(solution)/shard_map/all_to_all | solution.py:91
  121.9 4.7 all-to-all-start.2
  126.6 0.5 reduce-scatter.4.cloned.1.call-start
  127.2 2.7 slice_bitcast_fusion.1
  129.9 1.9 collective-permute-start.1
  131.7 2.9 slice_bitcast_fusion.2
  134.6 0.2 collective-permute-start
  134.8 5.4 slice.33
  140.1 2.6 slice.29
  142.7 0.2 slice-done.7
  143.0 2.6 slice.27
  145.6 0.7 fusion.34
  147.0 22.5 %collective-permute-done.2 = bf16[2048,384]{1,0:T(8,128)(2,1)} collective-permute-done((bf16[2048,384]{1,0:T(8,128)(2,1)}, bf16[2048,384]{1,0:T(8,128)(2,1)}, u32[]{:S(2)}, u32[]{:S(2)}) %collective-permute-start.2) | collective-permute-done | bytes 1572896 | tf_op jit(solution)/shard_map/ppermute | solution.py:10
  169.5 3.4 select_bitcast_fusion
  172.8 72.5 %collective-permute-done.1 = bf16[2048,384]{1,0:T(8,128)(2,1)} collective-permute-done((bf16[2048,384]{1,0:T(8,128)(2,1)}, bf16[2048,384]{1,0:T(8,128)(2,1)}, u32[]{:S(2)}, u32[]{:S(2)}) %collective-permute-start.1) | collective-permute-done | bytes 1572896 | tf_op jit(solution)/shard_map/ppermute | solution.py:10
  245.3 2.1 select_bitcast_fusion.1
  247.4 30.8 %collective-permute-done = bf16[2048,384]{1,0:T(8,128)(2,1)} collective-permute-done((bf16[2048,384]{1,0:T(8,128)(2,1)}, bf16[2048,384]{1,0:T(8,128)(2,1)}, u32[]{:S(2)}, u32[]{:S(2)}) %collective-permute-start) | collective-permute-done | bytes 1572896 | tf_op jit(solution)/shard_map/ppermute | solution.py:10
  278.1 3.4 select_bitcast_fusion.2
  281.5 7.2 %fusion.5 = f32[4,384,8,40]{1,3,2,0:T(8,128)} fusion(bf16[8,4,40,2048]{3,2,1,0:T(8,128)(2,1)} %all-to-all-done, bf16[1,2048,384]{2,1,0:T(8,128)(2,1)} %select_bitcast_fusion, bf16[3,2048,384]{2,1,0:T(8,128)(2,1)S(1)} %bitcast.131), kind=kOutput, calls=%fused_computation.22 | convolution fusion | flops 2025848832 | bytes 13500416 | tf_op jit(solution)/shard_map/nscd,sdf->nscf/dot_general | solution.py:25
  288.7 6.7 %fusion.7 = f32[4,384,8,40]{1,3,2,0:T(8,128)} fusion(bf16[8,4,40,2048]{3,2,1,0:T(8,128)(2,1)} %all-to-all-done, bf16[1,2048,384]{2,1,0:T(8,128)(2,1)S(1)} %select_bitcast_fusion.1, bf16[3,2048,384]{2,1,0:T(8,128)(2,1)S(1)} %bitcast.129), kind=kOutput, calls=%fused_computation.24 | convolution fusion | flops 2025848832 | bytes 13500416 | tf_op jit(solution)/shard_map/nscd,sdf->nscf/dot_general | solution.py:24
  295.4 10.2 %fusion.13 = (bf16[8,4,40,384]{3,2,0,1:T(8,128)(2,1)S(1)}, bf16[8,4,40,384]{3,2,0,1:T(8,128)(2,1)}, bf16[8,4,40,384]{3,2,0,1:T(8,128)(2,1)}) fusion(f32[4,384,8,40]{1,3,2,0:T(8,128)} %fusion.5, f32[4,384,8,40]{1,3,2,0:T(8,128)} %fusion.7, bf16[8,4,40,2048]{3,2,1,0:T(8,128)(2,1)} %all-to-all-done.2, bf16[1,2048,384]{2,1,0:T(8,128)(2,1)} %select_bitcast_fusion.2, ...), kind=kOutput, calls=%fused_computation.33 | convolution fusion | flops 2033713152 | bytes 18415616 | tf_op jit(solution)/shard_map/nscd,sdf->nscf/dot_general | solution.py:35
  305.5 9.3 %bitcast_convert_fusion.2 = bf16[4,2048,384]{2,1,0:T(8,128)(2,1)} fusion(bf16[8,4,40,2048]{3,2,1,0:T(8,128)(2,1)} %all-to-all-done, bf16[8,4,40,384]{3,2,0,1:T(8,128)(2,1)S(1)} %get-tuple-element.5), kind=kOutput, calls=%fused_computation.7 | convolution fusion | flops 2016411648 | bytes 12517376 | tf_op jit(solution)/shard_map/nscd,nscf->sdf/dot_general | solution.py:108
  314.9 0.0 reduce-scatter.6.cloned.1.call-start
  314.9 9.5 %bitcast_convert_fusion.1 = bf16[4,2048,384]{2,1,0:T(8,128)(2,1)} fusion(bf16[8,4,40,2048]{3,2,1,0:T(8,128)(2,1)} %all-to-all-done, bf16[8,4,40,384]{3,2,0,1:T(8,128)(2,1)} %get-tuple-element.7), kind=kOutput, calls=%fused_computation.6 | convolution fusion | flops 2016411648 | bytes 12517376 | tf_op jit(solution)/shard_map/nscd,nscf->sdf/dot_general | solution.py:109
  324.5 0.3 reduce-scatter.8.cloned.1.call-start
  324.7 9.4 %bitcast_convert_fusion = bf16[4,2048,384]{2,1,0:T(8,128)(2,1)} fusion(bf16[8,4,40,2048]{3,2,1,0:T(8,128)(2,1)} %all-to-all-done.2, bf16[8,4,40,384]{3,2,0,1:T(8,128)(2,1)} %get-tuple-element.6), kind=kOutput, calls=%fused_computation.5 | convolution fusion | flops 2016411648 | bytes 12517376 | tf_op jit(solution)/shard_map/nscd,nscf->sdf/dot_general | solution.py:110
  334.2 6.0 convert_bitcast_fusion
  340.2 2.7 copy.49
  342.9 5.0 all-to-all-start.1
  347.9 10.0 %fusion.9 = f32[4,2048,8,40]{1,3,2,0:T(8,128)} fusion(bf16[8,4,40,384]{3,2,0,1:T(8,128)(2,1)} %get-tuple-element.7, bf16[1,2048,384]{2,1,0:T(8,128)(2,1)} %select_bitcast_fusion, bf16[3,2048,384]{2,1,0:T(8,128)(2,1)} %slice.33), kind=kOutput, calls=%fused_computation.27 | convolution fusion | flops 2025848832 | bytes 17760256 | tf_op jit(solution)/shard_map/nscf,sdf->nscd/dot_general | solution.py:42
  357.9 10.6 %fusion.2 = bf16[8,4,40,2048]{3,2,0,1:T(8,128)(2,1)} fusion(f32[4,2048,8,40]{1,3,2,0:T(8,128)} %fusion.9, bf16[8,4,40,384]{3,2,0,1:T(8,128)(2,1)S(1)} %get-tuple-element.5, bf16[1,2048,384]{2,1,0:T(8,128)(2,1)S(1)} %select_bitcast_fusion.1, bf16[3,2048,384]{2,1,0:T(8,128)(2,1)} %slice.29), kind=kOutput, calls=%fused_computation.16 | convolution fusion | flops 2031091712 | bytes 23003136 | tf_op jit(solution)/shard_map/nscf,sdf->nscd/dot_general | solution.py:41
  368.5 5.6 copy.52
  374.1 34.1 %all-to-all-done.1 = bf16[8,4,40,2048]{3,2,1,0:T(8,128)(2,1)} async-done(((bf16[8,4,40,2048]{3,2,1,0:T(8,128)(2,1)}), bf16[8,4,40,2048]{3,2,1,0:T(8,128)(2,1)}, u32[]{:S(2)}, u32[]{:S(2)}) %all-to-all-start.1) | async-done | bytes 5242912 | tf_op jit(solution)/shard_map/all_to_all | solution.py:95
  408.2 5.0 all-to-all-start.3
  413.3 12.0 %gather_fusion.1 = bf16[1024,2048]{1,0:T(8,128)(2,1)} fusion(bf16[1280,2048]{1,0:T(8,128)(2,1)} %bitcast.20, s32[1024]{0:T(1024)S(1)} %broadcast_clamp_fusion), kind=kCustom, calls=%fused_computation.1 | custom fusion | bytes 8392704 | tf_op jit(solution)/shard_map/gather | solution.py:101
  425.3 48.3 %all-to-all-done.3 = bf16[8,4,40,2048]{3,2,1,0:T(8,128)(2,1)} async-done(((bf16[8,4,40,2048]{3,2,1,0:T(8,128)(2,1)}), bf16[8,4,40,2048]{3,2,1,0:T(8,128)(2,1)}, u32[]{:S(2)}, u32[]{:S(2)}) %all-to-all-start.3) | async-done | bytes 5242912 | tf_op jit(solution)/shard_map/all_to_all | solution.py:100
  473.6 12.1 %gather_fusion.3 = bf16[1024,2048]{1,0:T(8,128)(2,1)} fusion(bf16[1280,2048]{1,0:T(8,128)(2,1)} %bitcast.29, s32[1024]{0:T(1024)S(1)} %broadcast_clamp_fusion), kind=kCustom, calls=%fused_computation.3 | custom fusion | bytes 8392704 | tf_op jit(solution)/shard_map/gather | solution.py:105
  485.7 6.1 bitcast_reduce_fusion
  491.8 5.2 fusion
  496.9 43.8 %reduce-scatter.6.cloned.1.call-done = bf16[4,512,384]{2,1,0:T(8,128)(2,1)} async-done(((bf16[4,2048,384]{2,1,0:T(8,128)(2,1)}), bf16[4,512,384]{2,1,0:T(8,128)(2,1)}) %reduce-scatter.6.cloned.1.call-update) | async-done | bytes 1572880 | tf_op jit(solution)/shard_map/reduce_scatter | solution.py:116
  540.7 114.2 %reduce-scatter.8.cloned.1.call-done = bf16[4,512,384]{2,1,0:T(8,128)(2,1)} async-done(((bf16[4,2048,384]{2,1,0:T(8,128)(2,1)}), bf16[4,512,384]{2,1,0:T(8,128)(2,1)}) %reduce-scatter.8.cloned.1.call-update) | async-done | bytes 1572880 | tf_op jit(solution)/shard_map/reduce_scatter | solution.py:119
  (52 shorter events, 0.3 us)
Async XLA Ops:
  7.2 34.1 %copy-start = (bf16[128,2048]{1,0:T(8,128)(2,1)S(1)}, bf16[128,2048]{1,0:T(8,128)(2,1)}, u32[]{:S(2)}) copy-start(bf16[128,2048]{1,0:T(8,128)(2,1)} %param.8) | copy-start | bytes 1572868
  18.7 4.4 copy-start.5
  25.0 16.2 %copy-start.3 = (f32[128,8]{1,0:T(8,128)}, f32[128,8]{1,0:T(8,128)S(1)}, u32[]{:S(2)}) copy-start(f32[128,8]{1,0:T(8,128)S(1)} %copy.41) | copy-start | bytes 12292
  56.2 65.8 %all-to-all-start = ((bf16[8,4,40,2048]{3,2,1,0:T(8,128)(2,1)}), bf16[8,4,40,2048]{3,2,1,0:T(8,128)(2,1)}, u32[]{:S(2)}, u32[]{:S(2)}) async-start(bf16[8,4,40,2048]{3,2,1,0:T(8,128)(2,1)} %get-tuple-element.11), calls=%async_computation | async-start | bytes 10485760 | tf_op jit(solution)/shard_map/all_to_all | solution.py:91
  64.0 105.4 %collective-permute-start.2 = (bf16[2048,384]{1,0:T(8,128)(2,1)}, bf16[2048,384]{1,0:T(8,128)(2,1)}, u32[]{:S(2)}, u32[]{:S(2)}) collective-permute-start(bf16[2048,384]{1,0:T(8,128)(2,1)} %slice_bitcast_fusion), channel_id=1, source_target_pairs={{0,16},{4,20},{8,24},{12,28},{16,0},{20,4},{24,8},{28,12},{1,17},{... | collective-permute-start | bytes 4718600 | tf_op jit(solution)/shard_map/ppermute | solution.py:10
  121.9 173.4 %all-to-all-start.2 = ((bf16[8,4,40,2048]{3,2,1,0:T(8,128)(2,1)}), bf16[8,4,40,2048]{3,2,1,0:T(8,128)(2,1)}, u32[]{:S(2)}, u32[]{:S(2)}) async-start(bf16[8,4,40,2048]{3,2,1,0:T(8,128)(2,1)} %get-tuple-element.10), calls=%async_computation.2 | async-start | bytes 10485760 | tf_op jit(solution)/shard_map/all_to_all | solution.py:96
  126.6 370.3 %reduce-scatter.4.cloned.1.call-start = ((), (), s32[]{:S(2)}) async-start(), calls=%async_computation.7 | async-start | bytes 7864320 | tf_op jit(solution)/shard_map/reduce_scatter | solution.py:113
  129.9 115.4 %collective-permute-start.1 = (bf16[2048,384]{1,0:T(8,128)(2,1)}, bf16[2048,384]{1,0:T(8,128)(2,1)}, u32[]{:S(2)}, u32[]{:S(2)}) collective-permute-start(bf16[2048,384]{1,0:T(8,128)(2,1)} %slice_bitcast_fusion.1), channel_id=1, source_target_pairs={{0,16},{4,20},{8,24},{12,28},{16,0},{20,4},{24,8},{28,12},{1,17},{... | collective-permute-start | bytes 4718600 | tf_op jit(solution)/shard_map/ppermute | solution.py:10
  131.7 8.4 %slice-start.4 = ((s8[6291456]{0:T(1024)(128)(4,1)}), s8[2097152]{0:T(1024)(128)(4,1)S(1)}, s32[]{:S(2)}) async-start(s8[6291456]{0:T(1024)(128)(4,1)} %bitcast.132), calls=%async_computation.14 | async-start | bytes 4194304
  134.6 143.5 %collective-permute-start = (bf16[2048,384]{1,0:T(8,128)(2,1)}, bf16[2048,384]{1,0:T(8,128)(2,1)}, u32[]{:S(2)}, u32[]{:S(2)}) collective-permute-start(bf16[2048,384]{1,0:T(8,128)(2,1)} %slice_bitcast_fusion.2), channel_id=1, source_target_pairs={{0,16},{4,20},{8,24},{12,28},{16,0},{20,4},{24,8},{28,12},{1,17},{... | collective-permute-start | bytes 4718600 | tf_op jit(solution)/shard_map/ppermute | solution.py:10
  134.8 5.4 slice-start.5
  134.8 8.0 %slice-start.6 = ((s8[6291456]{0:T(1024)(128)(4,1)}), s8[4194304]{0:T(1024)(128)(4,1)S(1)}, s32[]{:S(2)}) async-start(s8[6291456]{0:T(1024)(128)(4,1)} %bitcast.134), calls=%async_computation.16 | async-start | bytes 8388608
  140.1 2.8 slice-start.7
  143.0 2.6 copy-start.7
  169.5 112.0 %slice-start.2 = ((s8[4718592]{0:T(1024)(128)(4,1)}), s8[4194304]{0:T(1024)(128)(4,1)S(1)}, s32[]{:S(2)}) async-start(s8[4718592]{0:T(1024)(128)(4,1)} %bitcast.130), calls=%async_computation.12 | async-start | bytes 8388608
  172.8 108.7 %slice-start.3 = ((s8[4718592]{0:T(1024)(128)(4,1)}), s8[524288]{0:T(1024)(128)(4,1)S(1)}, s32[]{:S(2)}) async-start(s8[4718592]{0:T(1024)(128)(4,1)} %bitcast.130), calls=%async_computation.13 | async-start | bytes 1048576
  278.1 10.5 %slice-start = ((s8[4718592]{0:T(1024)(128)(4,1)}), s8[4194304]{0:T(1024)(128)(4,1)S(1)}, s32[]{:S(2)}) async-start(s8[4718592]{0:T(1024)(128)(4,1)} %bitcast.128), calls=%async_computation.10 | async-start | bytes 8388608
  281.5 7.2 %slice-start.1 = ((s8[4718592]{0:T(1024)(128)(4,1)}), s8[524288]{0:T(1024)(128)(4,1)S(1)}, s32[]{:S(2)}) async-start(s8[4718592]{0:T(1024)(128)(4,1)} %bitcast.128), calls=%async_computation.11 | async-start | bytes 1048576
  314.9 225.9 %reduce-scatter.6.cloned.1.call-start = ((), (), s32[]{:S(2)}) async-start(), calls=%async_computation.8 | async-start | bytes 7864320 | tf_op jit(solution)/shard_map/reduce_scatter | solution.py:116
  324.5 330.5 %reduce-scatter.8.cloned.1.call-start = ((), (), s32[]{:S(2)}) async-start(), calls=%async_computation.9 | async-start | bytes 7864320 | tf_op jit(solution)/shard_map/reduce_scatter | solution.py:119
  342.9 65.3 %all-to-all-start.1 = ((bf16[8,4,40,2048]{3,2,1,0:T(8,128)(2,1)}), bf16[8,4,40,2048]{3,2,1,0:T(8,128)(2,1)}, u32[]{:S(2)}, u32[]{:S(2)}) async-start(bf16[8,4,40,2048]{3,2,1,0:T(8,128)(2,1)} %copy.49), calls=%async_computation.1 | async-start | bytes 10485760 | tf_op jit(solution)/shard_map/all_to_all | solution.py:95
  374.1 39.1 %copy-start.6 = (s32[1024,1]{0,1:T(1,128)S(1)}, s32[1024,1]{0,1:T(1,128)}, u32[]{:S(2)}) copy-start(s32[1024,1]{0,1:T(1,128)} %copy-done.5) | copy-start | bytes 12292
  408.2 65.4 %all-to-all-start.3 = ((bf16[8,4,40,2048]{3,2,1,0:T(8,128)(2,1)}), bf16[8,4,40,2048]{3,2,1,0:T(8,128)(2,1)}, u32[]{:S(2)}, u32[]{:S(2)}) async-start(bf16[8,4,40,2048]{3,2,1,0:T(8,128)(2,1)} %copy.52), calls=%async_computation.3 | async-start | bytes 10485760 | tf_op jit(solution)/shard_map/all_to_all | solution.py:100
  473.6 18.2 %copy-start.4 = (f32[128,8]{1,0:T(8,128)S(1)}, f32[128,8]{1,0:T(8,128)}, u32[]{:S(2)}) copy-start(f32[128,8]{1,0:T(8,128)} %copy-done.3) | copy-start | bytes 12292
  473.6 181.3 %copy-start.1 = (bf16[128,2048]{1,0:T(8,128)(2,1)S(1)}, bf16[128,2048]{1,0:T(8,128)(2,1)}, u32[]{:S(2)}) copy-start(bf16[128,2048]{1,0:T(8,128)(2,1)} %param.8) | copy-start | bytes 1572868
  485.7 6.1 copy-start.2
Sparse Core Ops, SparseCore 0:
  315.0 111.5 reduce-scatter.3
  429.5 111.2 reduce-scatter.5
  543.6 111.2 reduce-scatter.7
where the time goes:
time: 668 us; the launch traced here: 662 us
  waiting for transfers between devices  422 us (63%)
  matrix products  78.9 us (12%)
  local copies, waits for them, and re-layouts  78 us (12%)
  other arithmetic  43.2 us (6%)
  starting transfers between devices  25 us (4%)
  between operations  15.2 us (2%)
    ppermute x3, waiting for transfers between devices, partner(): return lax.ppermute(value, axis, pairs)  126 us
    reduce_scatter x1, waiting for transfers between devices, local(): lax.psum_scatter(partials[2].astype(jnp.bfloat16), 'dp', scatter_dimensio...  114 us
    all_to_all x1, waiting for transfers between devices, local(): lax.all_to_all(send_rows, 'expert', split_axis=0, concat_axis=0, tiled=True)  55.5 us
    all_to_all x1, waiting for transfers between devices, local(): lax.all_to_all(input_terms, 'expert', split_axis=0, concat_axis=0, tiled=...  48.3 us
    reduce_scatter x1, waiting for transfers between devices, local(): lax.psum_scatter(partials[1].astype(jnp.bfloat16), 'dp', scatter_dimensio...  43.8 us
    all_to_all x1, waiting for transfers between devices, local(): lax.all_to_all(expert_out, 'expert', split_axis=0, concat_axis=0, tiled=T...  34.1 us
    gather x1, local copies, waits for them, and re-layouts, local(): send_cot = jnp.where(filled, route_cot[safe_route], zero_bf).reshape(layout)  13.6 us
  transfers between devices with their start and end apart: 10, of which 8 were waited for; matrix products, arithmetic and copies ran while one was open for 20% of the time, Pallas kernels for 0%

commit v1 on v0

v1 whole, which is shorter than its diff:
```python
import jax
import jax.numpy as jnp
from jax import lax
from jax.experimental import pallas as pl
from jax.experimental.pallas import tpu as pltpu
from jax.sharding import PartitionSpec as P

F32 = jnp.float32
BF16 = jnp.bfloat16
VMEM_BYTES = 56 * 1024 * 1024


def dot(a, b, dims):
    return lax.dot_general(a, b, (dims, ((), ())), preferred_element_type=F32)


def forward_kernel(slot_ref, x_ref, wg_ref, wu_ref, wd_ref, out_ref, hid_ref, dgate_ref, dup_ref):
    x = x_ref[...]
    gate = dot(x, wg_ref[...], ((1,), (0,)))
    up = dot(x, wu_ref[...], ((1,), (0,)))
    s = jax.nn.sigmoid(gate)
    silu = gate * s
    hidden = (silu * up).astype(BF16)
    hid_ref[...] = hidden
    dgate_ref[...] = up * s * (1.0 + gate * (1.0 - s))
    dup_ref[...] = silu
    out_ref[...] = dot(hidden, wd_ref[...], ((1,), (1,))).astype(BF16)


def backward_kernel(
    slot_ref, c_ref, dgate_ref, dup_ref, wg_ref, wu_ref, wd_ref, term_ref, gc_ref, uc_ref
):
    hidden_cot = dot(c_ref[...], wd_ref[...], ((1,), (0,)))
    gate_cot = (hidden_cot * dgate_ref[...]).astype(BF16)
    up_cot = (hidden_cot * dup_ref[...]).astype(BF16)
    gc_ref[...] = gate_cot
    uc_ref[...] = up_cot
    term_ref[...] = (
        dot(gate_cot, wg_ref[...], ((1,), (1,))) + dot(up_cot, wu_ref[...], ((1,), (1,)))
    ).astype(BF16)


def grads_kernel(x_ref, c_ref, gc_ref, uc_ref, hid_ref, out_ref):
    x = x_ref[...]
    out_ref[0, 0] = dot(x, gc_ref[...], ((0,), (0,))).astype(BF16)
    out_ref[0, 1] = dot(x, uc_ref[...], ((0,), (0,))).astype(BF16)
    out_ref[0, 2] = dot(c_ref[...], hid_ref[...], ((0,), (0,))).astype(BF16)


def expert_forward(slot, x, w_gate, w_up, w_down):
    rows, width = x.shape
    feat = w_gate.shape[2]
    tile = rows // 4
    weight = pl.BlockSpec((None, width, feat), lambda i, s: (s[0], 0, 0))
    wide = pl.BlockSpec((tile, width), lambda i, s: (i, 0))
    thin = pl.BlockSpec((tile, feat), lambda i, s: (i, 0))
    return pl.pallas_call(
        forward_kernel,
        grid_spec=pltpu.PrefetchScalarGridSpec(
            num_scalar_prefetch=1,
            grid=(rows // tile,),
            in_specs=[wide, weight, weight, weight],
            out_specs=[wide, thin, thin, thin],
        ),
        out_shape=[
            jax.ShapeDtypeStruct((rows, width), BF16),
            jax.ShapeDtypeStruct((rows, feat), BF16),
            jax.ShapeDtypeStruct((rows, feat), F32),
            jax.ShapeDtypeStruct((rows, feat), F32),
        ],
        compiler_params=pltpu.CompilerParams(vmem_limit_bytes=VMEM_BYTES),
        cost_estimate=pl.CostEstimate(
            flops=6 * rows * width * feat,
            bytes_accessed=4 * rows * width + 6 * width * feat + 10 * rows * feat,
            transcendentals=rows * feat,
        ),
    )(slot, x, w_gate, w_up, w_down)


def expert_backward(slot, c, dgate, dup, w_gate, w_up, w_down):
    rows, width = c.shape
    feat = w_gate.shape[2]
    tile = rows // 4
    weight = pl.BlockSpec((None, width, feat), lambda i, s: (s[0], 0, 0))
    wide = pl.BlockSpec((tile, width), lambda i, s: (i, 0))
    thin = pl.BlockSpec((tile, feat), lambda i, s: (i, 0))
    return pl.pallas_call(
        backward_kernel,
        grid_spec=pltpu.PrefetchScalarGridSpec(
            num_scalar_prefetch=1,
            grid=(rows // tile,),
            in_specs=[wide, thin, thin, weight, weight, weight],
            out_specs=[wide, thin, thin],
        ),
        out_shape=[
            jax.ShapeDtypeStruct((rows, width), BF16),
            jax.ShapeDtypeStruct((rows, feat), BF16),
            jax.ShapeDtypeStruct((rows, feat), BF16),
        ],
        compiler_params=pltpu.CompilerParams(vmem_limit_bytes=VMEM_BYTES),
        cost_estimate=pl.CostEstimate(
            flops=6 * rows * width * feat,
            bytes_accessed=4 * rows * width + 6 * width * feat + 12 * rows * feat,
            transcendentals=0,
        ),
    )(slot, c, dgate, dup, w_gate, w_up, w_down)


def expert_grads(x, c, gate_cot, up_cot, hidden, parts):
    rows, width = x.shape
    feat = hidden.shape[1]
    cols = width // parts
    wide = pl.BlockSpec((rows, cols), lambda i: (0, i))
    thin = pl.BlockSpec((rows, feat), lambda i: (0, 0))
    return pl.pallas_call(
        grads_kernel,
        grid=(parts,),
        in_specs=[wide, wide, thin, thin, thin],
        out_specs=pl.BlockSpec((1, 3, cols, feat), lambda i: (i, 0, 0, 0)),
        out_shape=jax.ShapeDtypeStruct((parts, 3, cols, feat), BF16),
        compiler_params=pltpu.CompilerParams(vmem_limit_bytes=VMEM_BYTES),
        cost_estimate=pl.CostEstimate(
            flops=6 * rows * width * feat,
            bytes_accessed=4 * rows * width + 6 * width * feat + 6 * rows * feat,
            transcendentals=0,
        ),
    )(x, c, gate_cot, up_cot, hidden)


def local(tokens, cotangent, expert_ids, combine_weights, w_gate, w_up, w_down, swap_flags):
    tok_rows, width = tokens.shape
    top_count = expert_ids.shape[1]
    per_device = w_gate.shape[0]
    groups = lax.axis_size("expert")
    parts = lax.axis_size("dp")
    half = groups // 2
    experts_all = groups * per_device
    capacity = tok_rows * top_count * 5 // (4 * experts_all) * parts
    total = groups * capacity
    mine = lax.axis_index("dp")
    slot = mine.astype(jnp.int32).reshape(1)

    info = jnp.concatenate([expert_ids.astype(F32), combine_weights], axis=1)
    info = lax.all_gather(info, "dp", tiled=True)
    tok_all = lax.all_gather(tokens, "dp", tiled=True)
    cot_all = lax.all_gather(cotangent, "dp", tiled=True)
    ids = info[:, :top_count].astype(jnp.int32)
    weights = info[:, top_count:]
    count = ids.shape[0]
    wanted = jnp.arange(groups, dtype=jnp.int32) * per_device + mine
    match = ids[:, :, None] == wanted[None, None, :]
    hit = jnp.any(match, axis=1)
    route_weight = jnp.sum(jnp.where(match, weights[:, :, None], 0.0), axis=1)
    below = (jnp.arange(count)[:, None] > jnp.arange(count)[None, :]).astype(BF16)
    rank = dot(below, hit.astype(BF16), ((1,), (0,))).astype(jnp.int32)
    place = jnp.where(hit, rank, -1).T
    picked = place[:, None, :] == jnp.arange(capacity, dtype=jnp.int32)[None, :, None]
    row_weight = jnp.sum(jnp.where(picked, route_weight.T[:, None, :], 0.0), axis=2).reshape(total, 1)
    pick = picked.astype(BF16).reshape(total, count)
    pick_weighted = (
        jnp.where(picked, route_weight.T[:, None, :], 0.0).astype(BF16).reshape(total, count)
    )

    def exchange(value):
        shape = (groups, capacity, width)
        return lax.all_to_all(
            value.reshape(shape), "expert", split_axis=0, concat_axis=0, tiled=True
        ).reshape(total, width)

    x = exchange(dot(pick, tok_all, ((1,), (0,))).astype(BF16))
    c = exchange((dot(pick, cot_all, ((1,), (0,))) * row_weight).astype(BF16))
    out, hidden, dgate, dup = expert_forward(slot, x, w_gate, w_up, w_down)
    out_back = exchange(out)
    term, gate_cot, up_cot = expert_backward(slot, c, dgate, dup, w_gate, w_up, w_down)
    grads = expert_grads(x, c, gate_cot, up_cot, hidden, parts)
    grads = lax.all_to_all(grads, "dp", split_axis=0, concat_axis=0, tiled=True)
    term_back = exchange(term)

    mixed_part = dot(pick_weighted, out_back, ((0,), (0,))).astype(BF16)
    mixed = lax.psum_scatter(mixed_part, "dp", scatter_dimension=0, tiled=True)
    input_part = dot(pick, term_back, ((0,), (0,))).astype(BF16)
    input_grad = lax.psum_scatter(input_part, "dp", scatter_dimension=0, tiled=True)

    last = grads[per_device - 1]
    pairs = [(i, (i + half) % groups) for i in range(groups)]
    peer = lax.ppermute(last, "expert", pairs)
    pair = lax.axis_index("expert") % half
    flag = jnp.sum(jnp.where(jnp.arange(half) == pair, swap_flags, 0)) == 1
    chosen = jnp.where(flag, peer, last)
    out_grads = [
        jnp.concatenate([grads[: per_device - 1, m], chosen[None, m]], axis=0) for m in range(3)
    ]
    return (mixed, input_grad, *out_grads)


def solution(mesh):
    return jax.shard_map(
        local,
        mesh=mesh,
        in_specs=(
            P(("expert", "dp"), None),
            P(("expert", "dp"), None),
            P(("expert", "dp"), None),
            P(("expert", "dp"), None),
            P("expert", None, None),
            P("expert", None, None),
            P("expert", None, None),
            P(),
        ),
        out_specs=(
            P(("expert", "dp"), None),
            P(("expert", "dp"), None),
            P("expert", "dp", None),
            P("expert", "dp", None),
            P("expert", "dp", None),
        ),
        check_vma=False,
    )
```

time: 668 us -> 520 us (0.78)
  local copies, waits for them, and re-layouts: 78 us -> 4.06 us
  matrix products: 78.9 us -> 25.8 us
  waiting for transfers between devices: 422 us -> 379 us
  Pallas kernels: 0 us -> 39.4 us
  other arithmetic: 43.2 us -> 7.76 us
  blocking collectives: 0 us -> 14.9 us
    reduce_scatter x3 -> x2, waiting for transfers between devices: 158 us -> 0.01 us  [the longest x1 0.01 us: local(): mixed = lax.psum_scatter(mixed_part, 'dp', scatter_dimension=0, tiled=True)]
    all_to_all x4 -> x5, waiting for transfers between devices: 138 us -> 281 us  [the longest x4 148 us: exchange(): lax.all_to_all(value.reshape(shape), 'expert', split_axis=0, concat_axis=...]
    ppermute x3 -> x1, waiting for transfers between devices: 126 us -> 16.9 us  [local(): peer = lax.ppermute(last, 'expert', pairs)]
    all_gather x0 -> x2, waiting for transfers between devices: none -> 79.5 us  [the longest x1 46.2 us: local(): cot_all = lax.all_gather(cotangent, 'dp', tiled=True)]
    dot_general x9 -> x5, matrix products: 78.9 us -> 25.8 us  [dot(): return lax.dot_general(a, b, (dims, ((), ())), preferred_element_type=F32)]
    gather x4 -> x0, local copies, waits for them, and re-layouts: 43.8 us -> none  [the longest x1 13.6 us: local(): send_cot = jnp.where(filled, route_cot[safe_route], zero_bf).reshape(layout)]
    pallas_call x0 -> x3, Pallas kernels: none -> 39.4 us  [the longest x1 13.6 us: expert_backward(): pl.pallas_call(backward_kernel, grid_spec=pltpu.PrefetchScalarGridSpec(nu...]
    all_gather x0 -> x1, blocking collectives: none -> 14.9 us  [local(): info = lax.all_gather(info, 'dp', tiled=True)]
  transfers between devices with their start and end apart: 10 -> 10, of which waited for: 8 -> 8; matrix products, arithmetic and copies ran while one was open for 20% -> 6% of each run, Pallas kernels for 0% -> 8%
where the time goes in v1:
time: 520 us; the launch traced here: 511 us
  waiting for transfers between devices  379 us (73%)
  Pallas kernels  39.4 us (8%)
  matrix products  25.8 us (5%)
  starting transfers between devices  25.4 us (5%)
  blocking collectives  14.9 us (3%)
  between operations  14.5 us (3%)
  other arithmetic  7.76 us (1%)
    all_to_all x4, waiting for transfers between devices, exchange(): lax.all_to_all(value.reshape(shape), 'expert', split_axis=0, concat_axis=...  148 us
    all_to_all x1, waiting for transfers between devices, local(): grads = lax.all_to_all(grads, 'dp', split_axis=0, concat_axis=0, tiled=True)  133 us
    all_gather x1, waiting for transfers between devices, local(): cot_all = lax.all_gather(cotangent, 'dp', tiled=True)  46.2 us
    all_gather x1, waiting for transfers between devices, local(): tok_all = lax.all_gather(tokens, 'dp', tiled=True)  33.3 us
    dot_general x5, matrix products, dot(): return lax.dot_general(a, b, (dims, ((), ())), preferred_element_type=F32)  25.8 us
    all_to_all x4, starting transfers between devices, exchange(): lax.all_to_all(value.reshape(shape), 'expert', split_axis=0, concat_axis=...  18.6 us
    ppermute x1, waiting for transfers between devices, local(): peer = lax.ppermute(last, 'expert', pairs)  16.9 us
    all_gather x1, blocking collectives, local(): info = lax.all_gather(info, 'dp', tiled=True)  14.9 us
  transfers between devices with their start and end apart: 10, of which 8 were waited for; matrix products, arithmetic and copies ran while one was open for 6% of the time, Pallas kernels for 8%

profile of v1, /device:TPU:0, one launch (start us, length us, event | category | flops | bytes accessed | tf_op | source)
XLA Modules:
  0.0 511.1 jit_solution(12691556737303674483)
XLA Ops:
  7.2 0.0 all-gather.3.cloned.1.call-start
  7.2 0.7 all-gather.3.cloned.1.call-update
  7.9 0.1 eq.56
  8.0 0.7 convert_element_type.28
  8.7 0.7 pad_maximum_fusion.3
  9.4 14.9 %all_gather.9 = f32[512,16]{0,1:T(8,128)S(1)} all-gather(f32[128,16]{0,1:T(8,128)S(1)} %pad_maximum_fusion.3), channel_id=1, replica_groups=mesh['expert'=8,'dp'=4] {'dp'}, dimensions={0}, use_global_device_ids=true | all-gather | bytes 40960 | tf_op jit(solution)/shard_map/all_gather | solution.py:144
  24.3 0.1 compare_reduce_fusion
  24.4 0.2 fusion.4
  24.6 0.5 bitcast_compare_fusion
  25.0 33.3 %all-gather.3.cloned.1.call-done = bf16[512,2048]{1,0:T(8,128)(2,1)} async-done(((bf16[128,2048]{1,0:T(8,128)(2,1)}), bf16[512,2048]{1,0:T(8,128)(2,1)}) %all-gather.3.cloned.1.call-update) | async-done | bytes 2097168 | tf_op jit(solution)/shard_map/all_gather | solution.py:145
  58.3 6.2 %convolution_convert_fusion = bf16[1280,2048]{1,0:T(8,128)(2,1)} fusion(pred[1280,512]{1,0:T(32,128)(4,1)S(1)} %bitcast_compare_fusion, bf16[512,2048]{1,0:T(8,128)(2,1)} %all-gather.3.cloned.1.call-done), kind=kOutput, calls=%fused_computation.1 | convolution fusion | flops 2686976000 | bytes 7995392 | tf_op jit(solution)/shard_map/dot_general | solution.py:14
  64.5 4.6 all-to-all-start
  69.2 0.0 all-gather.5.cloned.1.call-start
  69.2 0.7 all-gather.5.cloned.1.call-update
  69.9 0.1 fusion.5
  70.0 0.4 select_reduce_fusion
  70.4 0.1 mul.18
  70.5 46.2 %all-gather.5.cloned.1.call-done = bf16[512,2048]{1,0:T(8,128)(2,1)} async-done(((bf16[128,2048]{1,0:T(8,128)(2,1)}), bf16[512,2048]{1,0:T(8,128)(2,1)}) %all-gather.5.cloned.1.call-update) | async-done | bytes 2097168 | tf_op jit(solution)/shard_map/all_gather | solution.py:146
  116.7 6.1 %multiply_convert_fusion = bf16[1280,2048]{1,0:T(8,128)(2,1)} fusion(pred[1280,512]{1,0:T(32,128)(4,1)S(1)} %bitcast_compare_fusion, bf16[512,2048]{1,0:T(8,128)(2,1)} %all-gather.5.cloned.1.call-done, f32[1280]{0:T(1024)S(1)} %mul.18), kind=kOutput, calls=%fused_computation | convolution fusion | flops 2689597440 | bytes 8000512 | tf_op jit(solution)/shard_map/dot_general | solution.py:14
  122.8 6.7 %all-to-all-done = bf16[8,160,2048]{2,1,0:T(8,128)(2,1)} async-done(((bf16[8,160,2048]{2,1,0:T(8,128)(2,1)}), bf16[8,160,2048]{2,1,0:T(8,128)(2,1)}, u32[]{:S(2)}, u32[]{:S(2)}) %all-to-all-start) | async-done | bytes 5242912 | tf_op jit(solution)/shard_map/all_to_all | solution.py:166
  129.5 4.7 all-to-all-start.2
  134.2 13.2 %shard_map.119 = (bf16[1280,2048]{1,0:T(8,128)(2,1)}, bf16[1280,384]{1,0:T(8,128)(2,1)}, f32[1280,384]{1,0:T(8,128)}, f32[1280,384]{1,0:T(8,128)}) custom-call(s32[1]{0:T(128)} %bitcast.2.slot_ref, bf16[1280,2048]{1,0:T(8,128)(2,1)} %bitcast.5.x_ref, bf16[4,2048,384]{2,1,0:T(8,128)(2,1)} %wg_ref.3, bf16[4,2048,384]{2,1,0:T(8,128)(2,1)} %wu_ref.3, ...), custom_call_target="tpu_custom_call" | custom-call | flops 6039797760 | bytes 20119552 | tf_op jit(solution)/shard_map/pallas_call | solution.py:57
  147.4 47.2 %all-to-all-done.2 = bf16[8,160,2048]{2,1,0:T(8,128)(2,1)} async-done(((bf16[8,160,2048]{2,1,0:T(8,128)(2,1)}), bf16[8,160,2048]{2,1,0:T(8,128)(2,1)}, u32[]{:S(2)}, u32[]{:S(2)}) %all-to-all-start.2) | async-done | bytes 5242912 | tf_op jit(solution)/shard_map/all_to_all | solution.py:166
  194.6 4.7 all-to-all-start.1
  199.3 13.6 %shard_map.120 = (bf16[1280,2048]{1,0:T(8,128)(2,1)}, bf16[1280,384]{1,0:T(8,128)(2,1)}, bf16[1280,384]{1,0:T(8,128)(2,1)}) custom-call(s32[1]{0:T(128)} %bitcast.2.slot_ref, bf16[1280,2048]{1,0:T(8,128)(2,1)} %bitcast.9.c_ref, f32[1280,384]{1,0:T(8,128)} %get-tuple-element.13.dgate_ref, f32[1280,384]{1,0:T(8,128)} %get-tuple-element.14.dup_ref, ...), custom_call_target="tpu_custom_call" | custom-call | flops 6039797760 | bytes 21102592 | tf_op jit(solution)/shard_map/pallas_call | solution.py:87
  212.9 46.7 %all-to-all-done.1 = bf16[8,160,2048]{2,1,0:T(8,128)(2,1)} async-done(((bf16[8,160,2048]{2,1,0:T(8,128)(2,1)}), bf16[8,160,2048]{2,1,0:T(8,128)(2,1)}, u32[]{:S(2)}, u32[]{:S(2)}) %all-to-all-start.1) | async-done | bytes 5242912 | tf_op jit(solution)/shard_map/all_to_all | solution.py:166
  259.6 4.7 all-to-all-start.3
  264.3 12.6 %shard_map.121 = bf16[4,3,512,384]{3,2,1,0:T(8,128)(2,1)} custom-call(bf16[1280,2048]{1,0:T(8,128)(2,1)} %bitcast.5.x_ref, bf16[1280,2048]{1,0:T(8,128)(2,1)} %bitcast.9.c_ref, bf16[1280,384]{1,0:T(8,128)(2,1)} %get-tuple-element.16.gc_ref, bf16[1280,384]{1,0:T(8,128)(2,1)} %get-tuple-element.17.uc_ref, bf16[1280,384]{1,0:T(8,128)(2,1)} %get-tuple-element.18.hid_ref), custom_call_target="tpu_custom_call" | custom-call | flops 6039797760 | bytes 18153472 | tf_op jit(solution)/shard_map/pallas_call | solution.py:115
  276.9 47.7 %all-to-all-done.3 = bf16[8,160,2048]{2,1,0:T(8,128)(2,1)} async-done(((bf16[8,160,2048]{2,1,0:T(8,128)(2,1)}), bf16[8,160,2048]{2,1,0:T(8,128)(2,1)}, u32[]{:S(2)}, u32[]{:S(2)}) %all-to-all-start.3) | async-done | bytes 5242912 | tf_op jit(solution)/shard_map/all_to_all | solution.py:166
  324.7 4.9 all-to-all-start.4
  329.6 0.0 reduce-scatter.3.cloned.1.call-start
  329.7 6.6 %bitcast_convert_fusion.1 = bf16[512,2048]{1,0:T(8,128)(2,1)} fusion(bf16[8,160,2048]{2,1,0:T(8,128)(2,1)} %all-to-all-done.1, f32[8,512]{1,0:T(8,128)S(1)} %bitcast.38, s32[8,512]{1,0:T(8,128)S(1)} %fusion.4), kind=kOutput, calls=%fused_computation.3 | convolution fusion | flops 2686713856 | bytes 7372800 | tf_op jit(solution)/shard_map/dot_general | solution.py:14
  336.3 0.0 reduce-scatter.3.cloned.1.call-update
  336.3 0.2 reduce-scatter.5.cloned.1.call-start
  336.5 6.7 %bitcast_convert_fusion = bf16[512,2048]{1,0:T(8,128)(2,1)} fusion(bf16[8,160,2048]{2,1,0:T(8,128)(2,1)} %all-to-all-done.3, s32[8,512]{1,0:T(8,128)S(1)} %fusion.4), kind=kOutput, calls=%fused_computation.2 | convolution fusion | flops 2686058496 | bytes 7356416 | tf_op jit(solution)/shard_map/dot_general | solution.py:14
  343.2 0.0 copy-start
  343.2 0.0 reduce-scatter.5.cloned.1.call-update
  343.2 133.1 %all-to-all-done.4 = bf16[4,3,512,384]{3,2,1,0:T(8,128)(2,1)} async-done(((bf16[4,3,512,384]{3,2,1,0:T(8,128)(2,1)}), bf16[4,3,512,384]{3,2,1,0:T(8,128)(2,1)}, u32[]{:S(2)}, u32[]{:S(2)}) %all-to-all-start.4) | async-done | bytes 4718624 | tf_op jit(solution)/shard_map/all_to_all | solution.py:176
  476.3 1.4 slice_bitcast_fusion.2
  477.7 1.5 collective-permute-start
  479.2 0.0 copy-done
  479.2 0.6 fusion.6
  480.4 2.4 slice_bitcast_fusion
  482.8 16.9 %collective-permute-done = bf16[3,512,384]{2,1,0:T(8,128)(2,1)S(1)} collective-permute-done((bf16[3,512,384]{2,1,0:T(8,128)(2,1)S(1)}, bf16[3,512,384]{2,1,0:T(8,128)(2,1)S(1)}, u32[]{:S(2)}, u32[]{:S(2)}) %collective-permute-start) | collective-permute-done | bytes 1179680 | tf_op jit(solution)/shard_map/ppermute | solution.py:186
  499.7 1.4 broadcast_select_fusion
  501.1 0.1 fusion.8
  501.3 1.3 pad_maximum_fusion.2
  502.6 2.0 pad_maximum_fusion
  504.6 0.0 reduce-scatter.3.cloned.1.call-done
  504.6 0.0 reduce-scatter.5.cloned.1.call-done
  (3 shorter events, 0.0 us)
Async XLA Ops:
  7.2 51.2 %all-gather.3.cloned.1.call-start = ((), (), s32[]{:S(2)}) async-start(), calls=%async_computation.7 | async-start | bytes 2621440 | tf_op jit(solution)/shard_map/all_gather | solution.py:145
  64.5 65.0 %all-to-all-start = ((bf16[8,160,2048]{2,1,0:T(8,128)(2,1)}), bf16[8,160,2048]{2,1,0:T(8,128)(2,1)}, u32[]{:S(2)}, u32[]{:S(2)}) async-start(bf16[8,160,2048]{2,1,0:T(8,128)(2,1)} %bitcast.33), calls=%async_computation | async-start | bytes 10485760 | tf_op jit(solution)/shard_map/all_to_all | solution.py:166
  69.2 47.5 %all-gather.5.cloned.1.call-start = ((), (), s32[]{:S(2)}) async-start(), calls=%async_computation.9 | async-start | bytes 2621440 | tf_op jit(solution)/shard_map/all_gather | solution.py:146
  129.5 65.1 %all-to-all-start.2 = ((bf16[8,160,2048]{2,1,0:T(8,128)(2,1)}), bf16[8,160,2048]{2,1,0:T(8,128)(2,1)}, u32[]{:S(2)}, u32[]{:S(2)}) async-start(bf16[8,160,2048]{2,1,0:T(8,128)(2,1)} %bitcast.36), calls=%async_computation.3 | async-start | bytes 10485760 | tf_op jit(solution)/shard_map/all_to_all | solution.py:166
  194.6 65.0 %all-to-all-start.1 = ((bf16[8,160,2048]{2,1,0:T(8,128)(2,1)}), bf16[8,160,2048]{2,1,0:T(8,128)(2,1)}, u32[]{:S(2)}, u32[]{:S(2)}) async-start(bf16[8,160,2048]{2,1,0:T(8,128)(2,1)} %bitcast.35), calls=%async_computation.1 | async-start | bytes 10485760 | tf_op jit(solution)/shard_map/all_to_all | solution.py:166
  259.6 65.0 %all-to-all-start.3 = ((bf16[8,160,2048]{2,1,0:T(8,128)(2,1)}), bf16[8,160,2048]{2,1,0:T(8,128)(2,1)}, u32[]{:S(2)}, u32[]{:S(2)}) async-start(bf16[8,160,2048]{2,1,0:T(8,128)(2,1)} %bitcast.34), calls=%async_computation.4 | async-start | bytes 10485760 | tf_op jit(solution)/shard_map/all_to_all | solution.py:166
  324.7 151.6 %all-to-all-start.4 = ((bf16[4,3,512,384]{3,2,1,0:T(8,128)(2,1)}), bf16[4,3,512,384]{3,2,1,0:T(8,128)(2,1)}, u32[]{:S(2)}, u32[]{:S(2)}) async-start(bf16[4,3,512,384]{3,2,1,0:T(8,128)(2,1)} %shard_map.121), calls=%async_computation.6 | async-start | bytes 9437184 | tf_op jit(solution)/shard_map/all_to_all | solution.py:176
  329.6 175.0 %reduce-scatter.3.cloned.1.call-start = ((), (), s32[]{:S(2)}) async-start(), calls=%async_computation.8 | async-start | bytes 2621440 | tf_op jit(solution)/shard_map/reduce_scatter | solution.py:180
  336.3 168.3 %reduce-scatter.5.cloned.1.call-start = ((), (), s32[]{:S(2)}) async-start(), calls=%async_computation.10 | async-start | bytes 2621440 | tf_op jit(solution)/shard_map/reduce_scatter | solution.py:182
  343.2 136.0 %copy-start = (s32[4]{0:T(128)S(1)}, s32[4]{0:T(128)}, u32[]{:S(2)}) copy-start(s32[4]{0:T(128)} %param.15) | copy-start | bytes 52
  477.7 22.0 %collective-permute-start = (bf16[3,512,384]{2,1,0:T(8,128)(2,1)S(1)}, bf16[3,512,384]{2,1,0:T(8,128)(2,1)S(1)}, u32[]{:S(2)}, u32[]{:S(2)}) collective-permute-start(bf16[3,512,384]{2,1,0:T(8,128)(2,1)S(1)} %slice_bitcast_fusion.2), channel_id=1, source_target_pairs={{0,16},{4,20},{8,24},{12,28},{16,0},{20,4},{24,8},{28,12},{1,17},{... | collective-permute-start | bytes 3538952 | tf_op jit(solution)/shard_map/ppermute | solution.py:186
Sparse Core Ops, SparseCore 0:
  9.6 48.7 all-gather.2
  71.6 45.0 all-gather.4
  336.4 75.1 reduce-scatter.2
  414.4 85.2 reduce-scatter.4

commit v2 on v1

--- a/solution.py
+++ b/solution.py
@@ -173,23 +173,33 @@
     out_back = exchange(out)
     term, gate_cot, up_cot = expert_backward(slot, c, dgate, dup, w_gate, w_up, w_down)
     grads = expert_grads(x, c, gate_cot, up_cot, hidden, parts)
-    grads = lax.all_to_all(grads, "dp", split_axis=0, concat_axis=0, tiled=True)
+    term, grads = lax.optimization_barrier((term, grads))
+    received = [lax.dynamic_index_in_dim(grads, mine, keepdims=False)]
+    for step in range(1, parts):
+        sent = lax.dynamic_index_in_dim(grads, mine ^ step, keepdims=False)
+        received.append(lax.ppermute(sent, "dp", [(i, i ^ step) for i in range(parts)]))
+    term, *early = lax.optimization_barrier((term, *received[:-1]))
     term_back = exchange(term)
+    term_back, final = lax.optimization_barrier((term_back, received[-1]))
+    received = [*early, final]
 
     mixed_part = dot(pick_weighted, out_back, ((0,), (0,))).astype(BF16)
     mixed = lax.psum_scatter(mixed_part, "dp", scatter_dimension=0, tiled=True)
     input_part = dot(pick, term_back, ((0,), (0,))).astype(BF16)
     input_grad = lax.psum_scatter(input_part, "dp", scatter_dimension=0, tiled=True)
 
-    last = grads[per_device - 1]
+    last = lax.select_n((per_device - 1) ^ mine, *received)
     pairs = [(i, (i + half) % groups) for i in range(groups)]
     peer = lax.ppermute(last, "expert", pairs)
     pair = lax.axis_index("expert") % half
     flag = jnp.sum(jnp.where(jnp.arange(half) == pair, swap_flags, 0)) == 1
     chosen = jnp.where(flag, peer, last)
-    out_grads = [
-        jnp.concatenate([grads[: per_device - 1, m], chosen[None, m]], axis=0) for m in range(3)
-    ]
+    out_grads = []
+    for m in range(3):
+        whole = jnp.zeros((per_device,) + last.shape[1:], BF16)
+        for step in range(parts):
+            whole = lax.dynamic_update_index_in_dim(whole, received[step][m], mine ^ step, 0)
+        out_grads.append(whole.at[per_device - 1].set(chosen[m]))
     return (mixed, input_grad, *out_grads)
 
 

time: 520 us -> 439 us (0.84); the launches traced: 511 us -> 438 us
  waiting for transfers between devices: 379 us -> 299 us
  local copies, waits for them, and re-layouts: 4.06 us -> 16.2 us
    all_to_all x1 -> x0, waiting for transfers between devices: 133 us -> none  [local(): grads = lax.all_to_all(grads, 'dp', split_axis=0, concat_axis=0, tiled=True)]
    ppermute x0 -> x3, waiting for transfers between devices: none -> 102 us  [local(): lax.ppermute(sent, 'dp', [(i, i ^ step) for i in range(parts)])]
    all_to_all x4, waiting for transfers between devices: 148 us -> 55.8 us  [exchange(): lax.all_to_all(value.reshape(shape), 'expert', split_axis=0, concat_axis=...]
    reduce_scatter x1, waiting for transfers between devices: 0.01 us -> 44.6 us  [local(): lax.psum_scatter(input_part, 'dp', scatter_dimension=0, tiled=True)]
    dynamic_update_slice x0 -> x6, local copies, waits for them, and re-layouts: none -> 6.73 us  [local(): lax.dynamic_update_index_in_dim(whole, received[step][m], mine ^ step, 0)]
  transfers between devices with their start and end apart: 10 -> 12, of which waited for: 8 -> 10; matrix products, arithmetic and copies ran while one was open for 6% -> 9% of each run, Pallas kernels for 8% -> 9%
where the time goes in v2:
time: 439 us; the launch traced here: 438 us
  waiting for transfers between devices  299 us (68%)
  Pallas kernels  39.4 us (9%)
  matrix products  26.2 us (6%)
  starting transfers between devices  23.5 us (5%)
  local copies, waits for them, and re-layouts  16.2 us (4%)
  blocking collectives  14.9 us (3%)
  between operations  14.6 us (3%)
  other arithmetic  4.69 us (1%)
    ppermute x3, waiting for transfers between devices, local(): lax.ppermute(sent, 'dp', [(i, i ^ step) for i in range(parts)])  102 us
    all_to_all x4, waiting for transfers between devices, exchange(): lax.all_to_all(value.reshape(shape), 'expert', split_axis=0, concat_axis=...  55.8 us
    all_gather x1, waiting for transfers between devices, local(): cot_all = lax.all_gather(cotangent, 'dp', tiled=True)  46.2 us
    reduce_scatter x1, waiting for transfers between devices, local(): lax.psum_scatter(input_part, 'dp', scatter_dimension=0, tiled=True)  44.6 us
    all_gather x1, waiting for transfers between devices, local(): tok_all = lax.all_gather(tokens, 'dp', tiled=True)  33.3 us
    dot_general x5, matrix products, dot(): return lax.dot_general(a, b, (dims, ((), ())), preferred_element_type=F32)  26.2 us
    all_to_all x4, starting transfers between devices, exchange(): lax.all_to_all(value.reshape(shape), 'expert', split_axis=0, concat_axis=...  18.6 us
    ppermute x1, waiting for transfers between devices, local(): peer = lax.ppermute(last, 'expert', pairs)  15.6 us
  transfers between devices with their start and end apart: 12, of which 10 were waited for; matrix products, arithmetic and copies ran while one was open for 9% of the time, Pallas kernels for 9%

profile of v2, /device:TPU:0, one launch (start us, length us, event | category | flops | bytes accessed | tf_op | source)
XLA Modules:
  0.0 438.3 jit_solution(11850158285088196836)
XLA Ops:
  7.2 0.0 all-gather.3.cloned.1.call-start
  7.2 0.7 all-gather.3.cloned.1.call-update
  7.9 0.1 eq.56
  8.0 0.7 convert_element_type.28
  8.7 0.7 pad_maximum_fusion
  9.4 14.9 %all_gather.9 = f32[512,16]{0,1:T(8,128)S(1)} all-gather(f32[128,16]{0,1:T(8,128)S(1)} %pad_maximum_fusion), channel_id=1, replica_groups=mesh['expert'=8,'dp'=4] {'dp'}, dimensions={0}, use_global_device_ids=true | all-gather | bytes 40960 | tf_op jit(solution)/shard_map/all_gather | solution.py:144
  24.3 0.1 compare_reduce_fusion
  24.4 0.2 fusion.3
  24.6 0.5 bitcast_compare_fusion
  25.0 0.0 copy-start
  25.1 33.3 %all-gather.3.cloned.1.call-done = bf16[512,2048]{1,0:T(8,128)(2,1)} async-done(((bf16[128,2048]{1,0:T(8,128)(2,1)}), bf16[512,2048]{1,0:T(8,128)(2,1)}) %all-gather.3.cloned.1.call-update) | async-done | bytes 2097168 | tf_op jit(solution)/shard_map/all_gather | solution.py:145
  58.3 6.1 %convolution_convert_fusion = bf16[1280,2048]{1,0:T(8,128)(2,1)} fusion(pred[1280,512]{1,0:T(32,128)(4,1)S(1)} %bitcast_compare_fusion, bf16[512,2048]{1,0:T(8,128)(2,1)} %all-gather.3.cloned.1.call-done), kind=kOutput, calls=%fused_computation.1 | convolution fusion | flops 2686976000 | bytes 7995392 | tf_op jit(solution)/shard_map/dot_general | solution.py:14
  64.4 4.6 %all-to-all-start = ((bf16[8,160,2048]{2,1,0:T(8,128)(2,1)}), bf16[8,160,2048]{2,1,0:T(8,128)(2,1)}, u32[]{:S(2)}, u32[]{:S(2)}) async-start(bf16[8,160,2048]{2,1,0:T(8,128)(2,1)} %bitcast.33), calls=%async_computation | async-start | bytes 10485760 | tf_op jit(solution)/shard_map/all_to_all | solution.py:166
  69.1 0.0 all-gather.5.cloned.1.call-start
  69.1 0.7 all-gather.5.cloned.1.call-update
  69.9 0.1 fusion.4
  69.9 0.0 copy-start.1
  70.0 0.4 select_reduce_fusion
  70.3 0.1 mul.18
  70.4 46.2 %all-gather.5.cloned.1.call-done = bf16[512,2048]{1,0:T(8,128)(2,1)} async-done(((bf16[128,2048]{1,0:T(8,128)(2,1)}), bf16[512,2048]{1,0:T(8,128)(2,1)}) %all-gather.5.cloned.1.call-update) | async-done | bytes 2097168 | tf_op jit(solution)/shard_map/all_gather | solution.py:146
  116.6 0.0 copy-done
  116.6 6.2 %multiply_convert_fusion = bf16[1280,2048]{1,0:T(8,128)(2,1)} fusion(pred[1280,512]{1,0:T(32,128)(4,1)S(1)} %bitcast_compare_fusion, bf16[512,2048]{1,0:T(8,128)(2,1)} %all-gather.5.cloned.1.call-done, f32[1280]{0:T(1024)S(1)} %mul.18), kind=kOutput, calls=%fused_computation | convolution fusion | flops 2689597440 | bytes 8000512 | tf_op jit(solution)/shard_map/dot_general | solution.py:14
  122.8 0.0 copy-done.1
  122.8 6.6 %all-to-all-done = bf16[8,160,2048]{2,1,0:T(8,128)(2,1)} async-done(((bf16[8,160,2048]{2,1,0:T(8,128)(2,1)}), bf16[8,160,2048]{2,1,0:T(8,128)(2,1)}, u32[]{:S(2)}, u32[]{:S(2)}) %all-to-all-start) | async-done | bytes 5242912 | tf_op jit(solution)/shard_map/all_to_all | solution.py:166
  129.5 4.7 %all-to-all-start.2 = ((bf16[8,160,2048]{2,1,0:T(8,128)(2,1)}), bf16[8,160,2048]{2,1,0:T(8,128)(2,1)}, u32[]{:S(2)}, u32[]{:S(2)}) async-start(bf16[8,160,2048]{2,1,0:T(8,128)(2,1)} %bitcast.34), calls=%async_computation.3 | async-start | bytes 10485760 | tf_op jit(solution)/shard_map/all_to_all | solution.py:166
  134.1 13.2 %shard_map.119 = (bf16[1280,2048]{1,0:T(8,128)(2,1)}, bf16[1280,384]{1,0:T(8,128)(2,1)}, f32[1280,384]{1,0:T(8,128)}, f32[1280,384]{1,0:T(8,128)}) custom-call(s32[1]{0:T(128)} %bitcast.2.slot_ref, bf16[1280,2048]{1,0:T(8,128)(2,1)} %bitcast.5.x_ref, bf16[4,2048,384]{2,1,0:T(8,128)(2,1)} %wg_ref.3, bf16[4,2048,384]{2,1,0:T(8,128)(2,1)} %wu_ref.3, ...), custom_call_target="tpu_custom_call" | custom-call | flops 6039797760 | bytes 20119552 | tf_op jit(solution)/shard_map/pallas_call | solution.py:57
  147.4 47.1 %all-to-all-done.2 = bf16[8,160,2048]{2,1,0:T(8,128)(2,1)} async-done(((bf16[8,160,2048]{2,1,0:T(8,128)(2,1)}), bf16[8,160,2048]{2,1,0:T(8,128)(2,1)}, u32[]{:S(2)}, u32[]{:S(2)}) %all-to-all-start.2) | async-done | bytes 5242912 | tf_op jit(solution)/shard_map/all_to_all | solution.py:166
  194.5 4.7 %all-to-all-start.1 = ((bf16[8,160,2048]{2,1,0:T(8,128)(2,1)}), bf16[8,160,2048]{2,1,0:T(8,128)(2,1)}, u32[]{:S(2)}, u32[]{:S(2)}) async-start(bf16[8,160,2048]{2,1,0:T(8,128)(2,1)} %bitcast.31), calls=%async_computation.1 | async-start | bytes 10485760 | tf_op jit(solution)/shard_map/all_to_all | solution.py:166
  199.2 13.5 %shard_map.120 = (bf16[1280,2048]{1,0:T(8,128)(2,1)}, bf16[1280,384]{1,0:T(8,128)(2,1)}, bf16[1280,384]{1,0:T(8,128)(2,1)}) custom-call(s32[1]{0:T(128)} %bitcast.2.slot_ref, bf16[1280,2048]{1,0:T(8,128)(2,1)} %bitcast.9.c_ref, f32[1280,384]{1,0:T(8,128)} %get-tuple-element.57.dgate_ref, f32[1280,384]{1,0:T(8,128)} %get-tuple-element.58.dup_ref, ...), custom_call_target="tpu_custom_call" | custom-call | flops 6039797760 | bytes 21102592 | tf_op jit(solution)/shard_map/pallas_call | solution.py:87
  212.7 12.6 %shard_map.121 = bf16[4,3,512,384]{3,2,1,0:T(8,128)(2,1)} custom-call(bf16[1280,2048]{1,0:T(8,128)(2,1)} %bitcast.5.x_ref, bf16[1280,2048]{1,0:T(8,128)(2,1)} %bitcast.9.c_ref, bf16[1280,384]{1,0:T(8,128)(2,1)} %get-tuple-element.60.gc_ref, bf16[1280,384]{1,0:T(8,128)(2,1)} %get-tuple-element.61.uc_ref, bf16[1280,384]{1,0:T(8,128)(2,1)} %get-tuple-element.62.hid_ref), custom_call_target="tpu_custom_call" | custom-call | flops 6039797760 | bytes 18153472 | tf_op jit(solution)/shard_map/pallas_call | solution.py:115
  225.3 3.9 dynamic-slice_bitcast_fusion
  229.2 0.0 collective-permute-start
  229.2 1.7 collective-permute-start.1
  230.8 51.3 %collective-permute-done = bf16[3,512,384]{2,1,0:T(8,128)(2,1)S(1)} collective-permute-done((bf16[3,512,384]{2,1,0:T(8,128)(2,1)S(1)}, bf16[3,512,384]{2,1,0:T(8,128)(2,1)S(1)}, u32[]{:S(2)}, u32[]{:S(2)}) %collective-permute-start) | collective-permute-done | bytes 1179680 | tf_op jit(solution)/shard_map/ppermute | solution.py:180
  282.2 1.4 collective-permute-done.1
  283.6 0.0 all-to-all-done.1
  283.6 4.7 %all-to-all-start.3 = ((bf16[8,160,2048]{2,1,0:T(8,128)(2,1)}), bf16[8,160,2048]{2,1,0:T(8,128)(2,1)}, u32[]{:S(2)}, u32[]{:S(2)}) async-start(bf16[8,160,2048]{2,1,0:T(8,128)(2,1)} %bitcast.32), calls=%async_computation.4 | async-start | bytes 10485760 | tf_op jit(solution)/shard_map/all_to_all | solution.py:166
  288.3 0.2 reduce-scatter.3.cloned.1.call-start
  288.5 6.6 %bitcast_convert_fusion = bf16[512,2048]{1,0:T(8,128)(2,1)} fusion(bf16[8,160,2048]{2,1,0:T(8,128)(2,1)} %all-to-all-done.1, f32[8,512]{1,0:T(8,128)} %bitcast.36, s32[8,512]{1,0:T(8,128)S(1)} %fusion.3), kind=kOutput, calls=%fused_computation.2 | convolution fusion | flops 2686713856 | bytes 7372800 | tf_op jit(solution)/shard_map/dot_general | solution.py:14
  295.1 0.0 reduce-scatter.3.cloned.1.call-update
  295.2 0.0 reduce-scatter.5.cloned.1.call-start
  295.2 2.2 collective-permute-start.2
  297.4 49.2 %collective-permute-done.2 = bf16[3,512,384]{2,1,0:T(8,128)(2,1)} collective-permute-done((bf16[3,512,384]{2,1,0:T(8,128)(2,1)}, bf16[3,512,384]{2,1,0:T(8,128)(2,1)}, u32[]{:S(2)}, u32[]{:S(2)}) %collective-permute-start.2) | collective-permute-done | bytes 1179680 | tf_op jit(solution)/shard_map/ppermute | solution.py:180
  346.6 2.1 all-to-all-done.3
  348.6 7.0 %convolution_convert_fusion.1 = bf16[512,2048]{1,0:T(8,128)(2,1)} fusion(pred[1280,512]{1,0:T(32,128)(4,1)} %copy-done, bf16[1280,2048]{1,0:T(8,128)(2,1)} %bitcast.14), kind=kOutput, calls=%fused_computation.5 | convolution fusion | flops 2685403136 | bytes 7995392 | tf_op jit(solution)/shard_map/dot_general | solution.py:14
  355.7 0.0 copy-start.2
  355.7 0.0 reduce-scatter.5.cloned.1.call-update
  355.7 0.6 copy-done.2
  356.3 0.6 fusion.5
  357.6 1.3 broadcast.61.clone
  358.9 0.8 slice_dynamic-update-slice_fusion.6
  359.7 1.5 select_select_fusion
  361.2 0.7 collective-permute-start.3
  361.8 1.3 broadcast.61.clone.1
  363.1 0.8 slice_dynamic-update-slice_fusion.10
  363.9 1.3 broadcast.61.clone.2
  365.2 0.8 slice_dynamic-update-slice_fusion.14
  366.0 1.0 slice_dynamic-update-slice_fusion.5
  367.0 1.0 slice_dynamic-update-slice_fusion.4
  368.1 2.3 slice_dynamic-update-slice_fusion.3
  370.4 15.6 %collective-permute-done.3 = bf16[3,512,384]{2,1,0:T(8,128)(2,1)S(1)} collective-permute-done((bf16[3,512,384]{2,1,0:T(8,128)(2,1)S(1)}, bf16[3,512,384]{2,1,0:T(8,128)(2,1)S(1)}, u32[]{:S(2)}, u32[]{:S(2)}) %collective-permute-start.3) | collective-permute-done | bytes 1179680 | tf_op jit(solution)/shard_map/ppermute | solution.py:193
  386.0 0.2 broadcast_select_fusion
  386.2 1.0 slice_dynamic-update-slice_fusion
  387.2 44.6 %reduce-scatter.5.cloned.1.call-done = bf16[128,2048]{1,0:T(8,128)(2,1)} async-done(((bf16[512,2048]{1,0:T(8,128)(2,1)}), bf16[128,2048]{1,0:T(8,128)(2,1)}) %reduce-scatter.5.cloned.1.call-update) | async-done | bytes 524304 | tf_op jit(solution)/shard_map/reduce_scatter | solution.py:189
  (4 shorter events, 0.0 us)
Async XLA Ops:
  7.2 51.2 %all-gather.3.cloned.1.call-start = ((), (), s32[]{:S(2)}) async-start(), calls=%async_computation.6 | async-start | bytes 2621440 | tf_op jit(solution)/shard_map/all_gather | solution.py:145
  25.0 91.6 %copy-start = (pred[1280,512]{1,0:T(32,128)(4,1)}, pred[1280,512]{1,0:T(32,128)(4,1)S(1)}, u32[]{:S(2)}) copy-start(pred[1280,512]{1,0:T(32,128)(4,1)S(1)} %bitcast_compare_fusion) | copy-start | bytes 1966084
  64.4 65.0 %all-to-all-start = ((bf16[8,160,2048]{2,1,0:T(8,128)(2,1)}), bf16[8,160,2048]{2,1,0:T(8,128)(2,1)}, u32[]{:S(2)}, u32[]{:S(2)}) async-start(bf16[8,160,2048]{2,1,0:T(8,128)(2,1)} %bitcast.33), calls=%async_computation | async-start | bytes 10485760 | tf_op jit(solution)/shard_map/all_to_all | solution.py:166
  69.1 47.5 %all-gather.5.cloned.1.call-start = ((), (), s32[]{:S(2)}) async-start(), calls=%async_computation.8 | async-start | bytes 2621440 | tf_op jit(solution)/shard_map/all_gather | solution.py:146
  69.9 52.9 %copy-start.1 = (f32[512,8]{0,1:T(8,128)}, f32[512,8]{0,1:T(8,128)S(1)}, u32[]{:S(2)}) copy-start(f32[512,8]{0,1:T(8,128)S(1)} %fusion.4) | copy-start | bytes 49156
  129.5 65.0 %all-to-all-start.2 = ((bf16[8,160,2048]{2,1,0:T(8,128)(2,1)}), bf16[8,160,2048]{2,1,0:T(8,128)(2,1)}, u32[]{:S(2)}, u32[]{:S(2)}) async-start(bf16[8,160,2048]{2,1,0:T(8,128)(2,1)} %bitcast.34), calls=%async_computation.3 | async-start | bytes 10485760 | tf_op jit(solution)/shard_map/all_to_all | solution.py:166
  194.5 89.1 %all-to-all-start.1 = ((bf16[8,160,2048]{2,1,0:T(8,128)(2,1)}), bf16[8,160,2048]{2,1,0:T(8,128)(2,1)}, u32[]{:S(2)}, u32[]{:S(2)}) async-start(bf16[8,160,2048]{2,1,0:T(8,128)(2,1)} %bitcast.31), calls=%async_computation.1 | async-start | bytes 10485760 | tf_op jit(solution)/shard_map/all_to_all | solution.py:166
  229.2 53.0 %collective-permute-start = (bf16[3,512,384]{2,1,0:T(8,128)(2,1)S(1)}, bf16[3,512,384]{2,1,0:T(8,128)(2,1)S(1)}, u32[]{:S(2)}, u32[]{:S(2)}) collective-permute-start(bf16[3,512,384]{2,1,0:T(8,128)(2,1)S(1)} %get-tuple-element.73), channel_id=1, source_target_pairs={{0,1},{1,0},{2,3},{3,2},{4,5},{5,4},{6,7},{7,6},{8,9},{9,8},{10,11... | collective-permute-start | bytes 3538952 | tf_op jit(solution)/shard_map/ppermute | solution.py:180
  229.2 54.4 %collective-permute-start.1 = (bf16[3,512,384]{2,1,0:T(8,128)(2,1)S(1)}, bf16[3,512,384]{2,1,0:T(8,128)(2,1)S(1)}, u32[]{:S(2)}, u32[]{:S(2)}) collective-permute-start(bf16[3,512,384]{2,1,0:T(8,128)(2,1)S(1)} %get-tuple-element.72), channel_id=1, source_target_pairs={{0,2},{1,3},{2,0},{3,1},{4,6},{5,7},{6,4},{7,5},{8,10},{9,11},{10,... | collective-permute-start | bytes 3538952 | tf_op jit(solution)/shard_map/ppermute | solution.py:180
  283.6 65.0 %all-to-all-start.3 = ((bf16[8,160,2048]{2,1,0:T(8,128)(2,1)}), bf16[8,160,2048]{2,1,0:T(8,128)(2,1)}, u32[]{:S(2)}, u32[]{:S(2)}) async-start(bf16[8,160,2048]{2,1,0:T(8,128)(2,1)} %bitcast.32), calls=%async_computation.4 | async-start | bytes 10485760 | tf_op jit(solution)/shard_map/all_to_all | solution.py:166
  288.3 98.9 %reduce-scatter.3.cloned.1.call-start = ((), (), s32[]{:S(2)}) async-start(), calls=%async_computation.7 | async-start | bytes 2621440 | tf_op jit(solution)/shard_map/reduce_scatter | solution.py:187
  295.2 136.6 %reduce-scatter.5.cloned.1.call-start = ((), (), s32[]{:S(2)}) async-start(), calls=%async_computation.9 | async-start | bytes 2621440 | tf_op jit(solution)/shard_map/reduce_scatter | solution.py:189
  295.2 51.4 %collective-permute-start.2 = (bf16[3,512,384]{2,1,0:T(8,128)(2,1)}, bf16[3,512,384]{2,1,0:T(8,128)(2,1)}, u32[]{:S(2)}, u32[]{:S(2)}) collective-permute-start(bf16[3,512,384]{2,1,0:T(8,128)(2,1)} %get-tuple-element.71), channel_id=1, source_target_pairs={{0,3},{1,2},{2,1},{3,0},{4,7},{5,6},{6,5},{7,4},{8,11},{9,10},{10,... | collective-permute-start | bytes 3538952 | tf_op jit(solution)/shard_map/ppermute | solution.py:180
  355.7 0.7 copy-start.2
  361.2 24.8 %collective-permute-start.3 = (bf16[3,512,384]{2,1,0:T(8,128)(2,1)S(1)}, bf16[3,512,384]{2,1,0:T(8,128)(2,1)S(1)}, u32[]{:S(2)}, u32[]{:S(2)}) collective-permute-start(bf16[3,512,384]{2,1,0:T(8,128)(2,1)S(1)} %select_select_fusion), channel_id=1, source_target_pairs={{0,16},{4,20},{8,24},{12,28},{16,0},{20,4},{24,8},{28,12},{1,17},{... | collective-permute-start | bytes 3538952 | tf_op jit(solution)/shard_map/ppermute | solution.py:193
Sparse Core Ops, SparseCore 0:
  9.6 48.7 all-gather.2
  71.5 45.0 all-gather.4
  295.3 73.7 reduce-scatter.2
  371.9 59.8 reduce-scatter.4

commit v3 on v2

--- a/solution.py
+++ b/solution.py
@@ -40,11 +40,11 @@
     ).astype(BF16)
 
 
-def grads_kernel(x_ref, c_ref, gc_ref, uc_ref, hid_ref, out_ref):
-    x = x_ref[...]
-    out_ref[0, 0] = dot(x, gc_ref[...], ((0,), (0,))).astype(BF16)
-    out_ref[0, 1] = dot(x, uc_ref[...], ((0,), (0,))).astype(BF16)
-    out_ref[0, 2] = dot(c_ref[...], hid_ref[...], ((0,), (0,))).astype(BF16)
+def grads_kernel(lhs_ref, *refs):
+    lhs = lhs_ref[...]
+    out_ref = refs[-1]
+    for k, right_ref in enumerate(refs[:-1]):
+        out_ref[0, k] = dot(lhs, right_ref[...], ((0,), (0,))).astype(BF16)
 
 
 def expert_forward(slot, x, w_gate, w_up, w_down):
@@ -106,25 +106,25 @@
     )(slot, c, dgate, dup, w_gate, w_up, w_down)
 
 
-def expert_grads(x, c, gate_cot, up_cot, hidden, parts):
-    rows, width = x.shape
-    feat = hidden.shape[1]
+def expert_grads(lhs, rights, parts):
+    rows, width = lhs.shape
+    feat = rights[0].shape[1]
+    number = len(rights)
     cols = width // parts
-    wide = pl.BlockSpec((rows, cols), lambda i: (0, i))
     thin = pl.BlockSpec((rows, feat), lambda i: (0, 0))
     return pl.pallas_call(
         grads_kernel,
         grid=(parts,),
-        in_specs=[wide, wide, thin, thin, thin],
-        out_specs=pl.BlockSpec((1, 3, cols, feat), lambda i: (i, 0, 0, 0)),
-        out_shape=jax.ShapeDtypeStruct((parts, 3, cols, feat), BF16),
+        in_specs=[pl.BlockSpec((rows, cols), lambda i: (0, i))] + [thin] * number,
+        out_specs=pl.BlockSpec((1, number, cols, feat), lambda i: (i, 0, 0, 0)),
+        out_shape=jax.ShapeDtypeStruct((parts, number, cols, feat), BF16),
         compiler_params=pltpu.CompilerParams(vmem_limit_bytes=VMEM_BYTES),
         cost_estimate=pl.CostEstimate(
-            flops=6 * rows * width * feat,
-            bytes_accessed=4 * rows * width + 6 * width * feat + 6 * rows * feat,
+            flops=2 * number * rows * width * feat,
+            bytes_accessed=2 * rows * width + 2 * number * (width + rows) * feat,
             transcendentals=0,
         ),
-    )(x, c, gate_cot, up_cot, hidden)
+    )(lhs, *rights)
 
 
 def local(tokens, cotangent, expert_ids, combine_weights, w_gate, w_up, w_down, swap_flags):
@@ -171,17 +171,28 @@
     c = exchange((dot(pick, cot_all, ((1,), (0,))) * row_weight).astype(BF16))
     out, hidden, dgate, dup = expert_forward(slot, x, w_gate, w_up, w_down)
     out_back = exchange(out)
+
+    def blocks(grads):
+        return [
+            lax.dynamic_index_in_dim(grads, mine ^ step, keepdims=False) for step in range(parts)
+        ]
+
+    def swap(block, step):
+        return lax.ppermute(block, "dp", [(i, i ^ step) for i in range(parts)])
+
+    down = blocks(expert_grads(c, [hidden], parts))
+    dgate, *down = lax.optimization_barrier((dgate, *down))
+    down = down[:1] + [swap(down[step], step) for step in range(1, parts)]
     term, gate_cot, up_cot = expert_backward(slot, c, dgate, dup, w_gate, w_up, w_down)
-    grads = expert_grads(x, c, gate_cot, up_cot, hidden, parts)
-    term, grads = lax.optimization_barrier((term, grads))
-    received = [lax.dynamic_index_in_dim(grads, mine, keepdims=False)]
-    for step in range(1, parts):
-        sent = lax.dynamic_index_in_dim(grads, mine ^ step, keepdims=False)
-        received.append(lax.ppermute(sent, "dp", [(i, i ^ step) for i in range(parts)]))
-    term, *early = lax.optimization_barrier((term, *received[:-1]))
+    both = blocks(expert_grads(x, [gate_cot, up_cot], parts))
+    both[0], *moved = lax.optimization_barrier((both[0], *both[1:], *down[1:]))
+    both, down = both[:1] + moved[: parts - 1], down[:1] + moved[parts - 1 :]
+    both = both[:1] + [swap(both[step], step) for step in range(1, parts)]
+    term, *ready = lax.optimization_barrier((term, *down, *both[:-1]))
     term_back = exchange(term)
-    term_back, final = lax.optimization_barrier((term_back, received[-1]))
-    received = [*early, final]
+    term_back, final = lax.optimization_barrier((term_back, both[-1]))
+    down, both = ready[:parts], [*ready[parts:], final]
+    received = [jnp.concatenate([b, d], axis=0) for b, d in zip(both, down)]
 
     mixed_part = dot(pick_weighted, out_back, ((0,), (0,))).astype(BF16)
     mixed = lax.psum_scatter(mixed_part, "dp", scatter_dimension=0, tiled=True)

time: 439 us -> 419 us (0.954)
  waiting for transfers between devices: 299 us -> 265 us
  starting transfers between devices: 23.5 us -> 34.5 us
    ppermute x3 -> x6, waiting for transfers between devices: 102 us -> 69 us  [swap(): return lax.ppermute(block, 'dp', [(i, i ^ step) for i in range(parts)])]
    reduce_scatter x1, waiting for transfers between devices: 44.6 us -> 27 us  [local(): lax.psum_scatter(input_part, 'dp', scatter_dimension=0, tiled=True)]
    all_to_all x4, waiting for transfers between devices: 55.8 us -> 72.5 us  [exchange(): lax.all_to_all(value.reshape(shape), 'expert', split_axis=0, concat_axis=...]
    ppermute x3 -> x6, starting transfers between devices: 3.83 us -> 14.9 us  [swap(): return lax.ppermute(block, 'dp', [(i, i ^ step) for i in range(parts)])]
    pallas_call x1 -> x2, Pallas kernels: 12.6 us -> 15.7 us  [expert_grads(): pl.pallas_call(grads_kernel, grid=(parts,), in_specs=[pl.BlockSpec((rows,...]
  transfers between devices with their start and end apart: 12 -> 15, of which waited for: 10 -> 10; matrix products, arithmetic and copies ran while one was open for 9% -> 10% of each run, Pallas kernels for 9% -> 10%
where the time goes in v3:
time: 419 us; the launch traced here: 418 us
  waiting for transfers between devices  265 us (63%)
  Pallas kernels  42.4 us (10%)
  starting transfers between devices  34.5 us (8%)
  matrix products  26.2 us (6%)
  local copies, waits for them, and re-layouts  17.1 us (4%)
  blocking collectives  14.9 us (4%)
  between operations  14.6 us (3%)
    all_to_all x4, waiting for transfers between devices, exchange(): lax.all_to_all(value.reshape(shape), 'expert', split_axis=0, concat_axis=...  72.5 us
    ppermute x6, waiting for transfers between devices, swap(): return lax.ppermute(block, 'dp', [(i, i ^ step) for i in range(parts)])  69 us
    all_gather x1, waiting for transfers between devices, local(): cot_all = lax.all_gather(cotangent, 'dp', tiled=True)  46.2 us
    all_gather x1, waiting for transfers between devices, local(): tok_all = lax.all_gather(tokens, 'dp', tiled=True)  33.3 us
    reduce_scatter x1, waiting for transfers between devices, local(): lax.psum_scatter(input_part, 'dp', scatter_dimension=0, tiled=True)  27 us
    dot_general x5, matrix products, dot(): return lax.dot_general(a, b, (dims, ((), ())), preferred_element_type=F32)  26.2 us
    all_to_all x4, starting transfers between devices, exchange(): lax.all_to_all(value.reshape(shape), 'expert', split_axis=0, concat_axis=...  18.7 us
    pallas_call x2, Pallas kernels, expert_grads(): pl.pallas_call(grads_kernel, grid=(parts,), in_specs=[pl.BlockSpec((rows,...  15.7 us
  transfers between devices with their start and end apart: 15, of which 10 were waited for; matrix products, arithmetic and copies ran while one was open for 10% of the time, Pallas kernels for 10%

profile of v3, /device:TPU:0, one launch (start us, length us, event | category | flops | bytes accessed | tf_op | source)
XLA Modules:
  0.0 418.3 jit_solution(16391029057089437433)
XLA Ops:
  7.2 0.0 all-gather.3.cloned.1.call-start
  7.2 0.7 all-gather.3.cloned.1.call-update
  7.9 0.1 eq.56
  8.0 0.7 convert_element_type.28
  8.7 0.7 pad_maximum_fusion
  9.4 14.9 %all_gather.9 = f32[512,16]{0,1:T(8,128)S(1)} all-gather(f32[128,16]{0,1:T(8,128)S(1)} %pad_maximum_fusion), channel_id=1, replica_groups=mesh['expert'=8,'dp'=4] {'dp'}, dimensions={0}, use_global_device_ids=true | all-gather | bytes 40960 | tf_op jit(solution)/shard_map/all_gather | solution.py:144
  24.3 0.1 compare_reduce_fusion
  24.4 0.2 fusion.4
  24.6 0.5 bitcast_compare_fusion
  25.1 33.3 %all-gather.3.cloned.1.call-done = bf16[512,2048]{1,0:T(8,128)(2,1)} async-done(((bf16[128,2048]{1,0:T(8,128)(2,1)}), bf16[512,2048]{1,0:T(8,128)(2,1)}) %all-gather.3.cloned.1.call-update) | async-done | bytes 2097168 | tf_op jit(solution)/shard_map/all_gather | solution.py:145
  58.3 6.1 %convolution_convert_fusion = bf16[1280,2048]{1,0:T(8,128)(2,1)} fusion(pred[1280,512]{1,0:T(32,128)(4,1)S(1)} %bitcast_compare_fusion, bf16[512,2048]{1,0:T(8,128)(2,1)} %all-gather.3.cloned.1.call-done), kind=kOutput, calls=%fused_computation.1 | convolution fusion | flops 2686976000 | bytes 7995392 | tf_op jit(solution)/shard_map/dot_general | solution.py:14
  64.5 4.7 %all-to-all-start = ((bf16[8,160,2048]{2,1,0:T(8,128)(2,1)}), bf16[8,160,2048]{2,1,0:T(8,128)(2,1)}, u32[]{:S(2)}, u32[]{:S(2)}) async-start(bf16[8,160,2048]{2,1,0:T(8,128)(2,1)} %bitcast.41), calls=%async_computation | async-start | bytes 10485760 | tf_op jit(solution)/shard_map/all_to_all | solution.py:166
  69.1 0.0 all-gather.5.cloned.1.call-start
  69.2 0.7 all-gather.5.cloned.1.call-update
  69.9 0.1 fusion.5
  70.0 0.4 select_reduce_fusion
  70.3 0.1 mul.18
  70.4 46.2 %all-gather.5.cloned.1.call-done = bf16[512,2048]{1,0:T(8,128)(2,1)} async-done(((bf16[128,2048]{1,0:T(8,128)(2,1)}), bf16[512,2048]{1,0:T(8,128)(2,1)}) %all-gather.5.cloned.1.call-update) | async-done | bytes 2097168 | tf_op jit(solution)/shard_map/all_gather | solution.py:146
  116.6 6.3 %multiply_convert_fusion = bf16[1280,2048]{1,0:T(8,128)(2,1)} fusion(pred[1280,512]{1,0:T(32,128)(4,1)S(1)} %bitcast_compare_fusion, bf16[512,2048]{1,0:T(8,128)(2,1)} %all-gather.5.cloned.1.call-done, f32[1280]{0:T(1024)S(1)} %mul.18), kind=kOutput, calls=%fused_computation | convolution fusion | flops 2689597440 | bytes 8000512 | tf_op jit(solution)/shard_map/dot_general | solution.py:14
  122.9 6.6 %all-to-all-done = bf16[8,160,2048]{2,1,0:T(8,128)(2,1)} async-done(((bf16[8,160,2048]{2,1,0:T(8,128)(2,1)}), bf16[8,160,2048]{2,1,0:T(8,128)(2,1)}, u32[]{:S(2)}, u32[]{:S(2)}) %all-to-all-start) | async-done | bytes 5242912 | tf_op jit(solution)/shard_map/all_to_all | solution.py:166
  129.5 4.7 %all-to-all-start.2 = ((bf16[8,160,2048]{2,1,0:T(8,128)(2,1)}), bf16[8,160,2048]{2,1,0:T(8,128)(2,1)}, u32[]{:S(2)}, u32[]{:S(2)}) async-start(bf16[8,160,2048]{2,1,0:T(8,128)(2,1)} %bitcast.42), calls=%async_computation.3 | async-start | bytes 10485760 | tf_op jit(solution)/shard_map/all_to_all | solution.py:166
  134.2 13.2 %shard_map.119 = (bf16[1280,2048]{1,0:T(8,128)(2,1)}, bf16[1280,384]{1,0:T(8,128)(2,1)}, f32[1280,384]{1,0:T(8,128)}, f32[1280,384]{1,0:T(8,128)}) custom-call(s32[1]{0:T(128)} %bitcast.2.slot_ref, bf16[1280,2048]{1,0:T(8,128)(2,1)} %bitcast.5.x_ref.lhs_ref, bf16[4,2048,384]{2,1,0:T(8,128)(2,1)} %wg_ref.3, bf16[4,2048,384]{2,1,0:T(8,128)(2,1)} %wu_ref.3, ...), custom_call_target="tpu_custom_call" | custom-call | flops 6039797760 | bytes 20119552 | tf_op jit(solution)/shard_map/pallas_call | solution.py:57
  147.4 47.2 %all-to-all-done.2 = bf16[8,160,2048]{2,1,0:T(8,128)(2,1)} async-done(((bf16[8,160,2048]{2,1,0:T(8,128)(2,1)}), bf16[8,160,2048]{2,1,0:T(8,128)(2,1)}, u32[]{:S(2)}, u32[]{:S(2)}) %all-to-all-start.2) | async-done | bytes 5242912 | tf_op jit(solution)/shard_map/all_to_all | solution.py:166
  194.5 4.7 %all-to-all-start.1 = ((bf16[8,160,2048]{2,1,0:T(8,128)(2,1)}), bf16[8,160,2048]{2,1,0:T(8,128)(2,1)}, u32[]{:S(2)}, u32[]{:S(2)}) async-start(bf16[8,160,2048]{2,1,0:T(8,128)(2,1)} %bitcast.39), calls=%async_computation.1 | async-start | bytes 10485760 | tf_op jit(solution)/shard_map/all_to_all | solution.py:166
  199.2 6.6 %shard_map.120 = bf16[4,1,512,384]{3,2,1,0:T(8,128)(2,1)} custom-call(bf16[1280,2048]{1,0:T(8,128)(2,1)} %bitcast.9.lhs_ref.c_ref, bf16[1280,384]{1,0:T(8,128)(2,1)} %get-tuple-element.72.refs_0_), custom_call_target="tpu_custom_call" | custom-call | flops 2013265920 | bytes 7798784 | tf_op jit(solution)/shard_map/pallas_call | solution.py:115
  205.8 1.5 dynamic-slice_bitcast_fusion.4
  207.3 0.1 collective-permute-start
  207.4 1.6 collective-permute-start.1
  209.0 2.7 collective-permute-start.2
  211.8 13.5 %shard_map.121 = (bf16[1280,2048]{1,0:T(8,128)(2,1)}, bf16[1280,384]{1,0:T(8,128)(2,1)}, bf16[1280,384]{1,0:T(8,128)(2,1)}) custom-call(s32[1]{0:T(128)} %bitcast.2.slot_ref, bf16[1280,2048]{1,0:T(8,128)(2,1)} %bitcast.9.lhs_ref.c_ref, f32[1280,384]{1,0:T(8,128)} %get-tuple-element.73.dgate_ref, f32[1280,384]{1,0:T(8,128)} %get-tuple-element.74.dup_ref, ...), custom_call_target="tpu_custom_call" | custom-call | flops 6039797760 | bytes 21102592 | tf_op jit(solution)/shard_map/pallas_call | solution.py:87
  225.3 9.1 %shard_map.122 = bf16[4,2,512,384]{3,2,1,0:T(8,128)(2,1)} custom-call(bf16[1280,2048]{1,0:T(8,128)(2,1)} %bitcast.5.x_ref.lhs_ref, bf16[1280,384]{1,0:T(8,128)(2,1)} %get-tuple-element.77.refs_0_, bf16[1280,384]{1,0:T(8,128)(2,1)} %get-tuple-element.78.refs_1_), custom_call_target="tpu_custom_call" | custom-call | flops 4026531840 | bytes 10354688 | tf_op jit(solution)/shard_map/pallas_call | solution.py:115
  234.4 3.1 dynamic-slice_bitcast_fusion
  237.5 8.1 %collective-permute-start.3 = (bf16[2,512,384]{2,1,0:T(8,128)(2,1)S(1)}, bf16[2,512,384]{2,1,0:T(8,128)(2,1)S(1)}, u32[]{:S(2)}, u32[]{:S(2)}) collective-permute-start(bf16[2,512,384]{2,1,0:T(8,128)(2,1)S(1)} %get-tuple-element.86), channel_id=1, source_target_pairs={{0,1},{1,0},{2,3},{3,2},{4,5},{5,4},{6,7},{7,6},{8,9},{9,8},{10,11... | collective-permute-start | bytes 2359304 | tf_op jit(solution)/shard_map/ppermute | solution.py:181
  245.6 0.6 collective-permute-start.4
  246.2 32.8 %collective-permute-done.3 = bf16[2,512,384]{2,1,0:T(8,128)(2,1)S(1)} collective-permute-done((bf16[2,512,384]{2,1,0:T(8,128)(2,1)S(1)}, bf16[2,512,384]{2,1,0:T(8,128)(2,1)S(1)}, u32[]{:S(2)}, u32[]{:S(2)}) %collective-permute-start.3) | collective-permute-done | bytes 786464 | tf_op jit(solution)/shard_map/ppermute | solution.py:181
  278.9 3.3 collective-permute-done.4
  282.2 4.7 %all-to-all-start.3 = ((bf16[8,160,2048]{2,1,0:T(8,128)(2,1)}), bf16[8,160,2048]{2,1,0:T(8,128)(2,1)}, u32[]{:S(2)}, u32[]{:S(2)}) async-start(bf16[8,160,2048]{2,1,0:T(8,128)(2,1)} %bitcast.40), calls=%async_computation.4 | async-start | bytes 10485760 | tf_op jit(solution)/shard_map/all_to_all | solution.py:166
  286.9 0.2 reduce-scatter.3.cloned.1.call-start
  287.1 6.6 %bitcast_convert_fusion = bf16[512,2048]{1,0:T(8,128)(2,1)} fusion(bf16[8,160,2048]{2,1,0:T(8,128)(2,1)} %all-to-all-done.1, f32[8,512]{1,0:T(8,128)S(1)} %bitcast.44, s32[8,512]{1,0:T(8,128)S(1)} %fusion.4), kind=kOutput, calls=%fused_computation.2 | convolution fusion | flops 2686713856 | bytes 7372800 | tf_op jit(solution)/shard_map/dot_general | solution.py:14
  293.8 0.0 reduce-scatter.3.cloned.1.call-update
  293.8 0.0 reduce-scatter.5.cloned.1.call-start
  293.8 1.8 collective-permute-start.5
  295.6 32.9 %collective-permute-done.5 = bf16[2,512,384]{2,1,0:T(8,128)(2,1)S(1)} collective-permute-done((bf16[2,512,384]{2,1,0:T(8,128)(2,1)}, bf16[2,512,384]{2,1,0:T(8,128)(2,1)S(1)}, u32[]{:S(2)}, u32[]{:S(2)}) %collective-permute-start.5) | collective-permute-done | bytes 786464 | tf_op jit(solution)/shard_map/ppermute | solution.py:181
  328.6 18.7 %all-to-all-done.3 = bf16[8,160,2048]{2,1,0:T(8,128)(2,1)} async-done(((bf16[8,160,2048]{2,1,0:T(8,128)(2,1)}), bf16[8,160,2048]{2,1,0:T(8,128)(2,1)}, u32[]{:S(2)}, u32[]{:S(2)}) %all-to-all-start.3) | async-done | bytes 5242912 | tf_op jit(solution)/shard_map/all_to_all | solution.py:166
  347.3 7.0 %convolution_convert_fusion.1 = bf16[512,2048]{1,0:T(8,128)(2,1)} fusion(pred[1280,512]{1,0:T(32,128)(4,1)} %copy-done.6, bf16[1280,2048]{1,0:T(8,128)(2,1)} %bitcast.19), kind=kOutput, calls=%fused_computation.5 | convolution fusion | flops 2685403136 | bytes 7995392 | tf_op jit(solution)/shard_map/dot_general | solution.py:14
  354.3 0.6 copy-done.7
  354.9 0.6 fusion.6
  356.2 1.3 broadcast.61.clone
  357.5 0.8 slice_dynamic-update-slice_fusion.6
  358.3 0.4 fusion.3
  358.7 0.6 collective-permute-start.6
  359.3 1.3 broadcast.61.clone.1
  360.6 0.8 slice_dynamic-update-slice_fusion.10
  361.4 1.3 broadcast.61.clone.2
  362.7 0.8 constant_dynamic-update-slice_fusion.3
  363.4 1.0 slice_dynamic-update-slice_fusion.5
  364.5 0.8 constant_dynamic-update-slice_fusion.1
  365.3 0.8 constant_dynamic-update-slice_fusion
  366.1 1.0 slice_dynamic-update-slice_fusion.4
  367.0 1.0 slice_dynamic-update-slice_fusion.3
  368.0 15.5 %collective-permute-done.6 = bf16[3,512,384]{2,1,0:T(8,128)(2,1)S(1)} collective-permute-done((bf16[3,512,384]{2,1,0:T(8,128)(2,1)S(1)}, bf16[3,512,384]{2,1,0:T(8,128)(2,1)S(1)}, u32[]{:S(2)}, u32[]{:S(2)}) %collective-permute-start.6) | collective-permute-done | bytes 1179680 | tf_op jit(solution)/shard_map/ppermute | solution.py:204
  383.5 0.2 broadcast_select_fusion
  383.7 1.0 slice_dynamic-update-slice_fusion
  384.7 27.0 %reduce-scatter.5.cloned.1.call-done = bf16[128,2048]{1,0:T(8,128)(2,1)} async-done(((bf16[512,2048]{1,0:T(8,128)(2,1)}), bf16[128,2048]{1,0:T(8,128)(2,1)}) %reduce-scatter.5.cloned.1.call-update) | async-done | bytes 524304 | tf_op jit(solution)/shard_map/reduce_scatter | solution.py:200
  (24 shorter events, 0.1 us)
Async XLA Ops:
  7.2 51.2 %all-gather.3.cloned.1.call-start = ((), (), s32[]{:S(2)}) async-start(), calls=%async_computation.6 | async-start | bytes 2621440 | tf_op jit(solution)/shard_map/all_gather | solution.py:145
  25.0 91.6 %copy-start.6 = (pred[1280,512]{1,0:T(32,128)(4,1)}, pred[1280,512]{1,0:T(32,128)(4,1)S(1)}, u32[]{:S(2)}) copy-start(pred[1280,512]{1,0:T(32,128)(4,1)S(1)} %bitcast_compare_fusion) | copy-start | bytes 1966084
  64.5 65.0 %all-to-all-start = ((bf16[8,160,2048]{2,1,0:T(8,128)(2,1)}), bf16[8,160,2048]{2,1,0:T(8,128)(2,1)}, u32[]{:S(2)}, u32[]{:S(2)}) async-start(bf16[8,160,2048]{2,1,0:T(8,128)(2,1)} %bitcast.41), calls=%async_computation | async-start | bytes 10485760 | tf_op jit(solution)/shard_map/all_to_all | solution.py:166
  69.1 47.5 %all-gather.5.cloned.1.call-start = ((), (), s32[]{:S(2)}) async-start(), calls=%async_computation.8 | async-start | bytes 2621440 | tf_op jit(solution)/shard_map/all_gather | solution.py:146
  129.5 65.0 %all-to-all-start.2 = ((bf16[8,160,2048]{2,1,0:T(8,128)(2,1)}), bf16[8,160,2048]{2,1,0:T(8,128)(2,1)}, u32[]{:S(2)}, u32[]{:S(2)}) async-start(bf16[8,160,2048]{2,1,0:T(8,128)(2,1)} %bitcast.42), calls=%async_computation.3 | async-start | bytes 10485760 | tf_op jit(solution)/shard_map/all_to_all | solution.py:166
  194.5 87.7 %all-to-all-start.1 = ((bf16[8,160,2048]{2,1,0:T(8,128)(2,1)}), bf16[8,160,2048]{2,1,0:T(8,128)(2,1)}, u32[]{:S(2)}, u32[]{:S(2)}) async-start(bf16[8,160,2048]{2,1,0:T(8,128)(2,1)} %bitcast.39), calls=%async_computation.1 | async-start | bytes 10485760 | tf_op jit(solution)/shard_map/all_to_all | solution.py:166
  207.3 30.1 %collective-permute-start = (bf16[1,512,384]{2,1,0:T(8,128)(2,1)S(1)}, bf16[1,512,384]{2,1,0:T(8,128)(2,1)S(1)}, u32[]{:S(2)}, u32[]{:S(2)}) collective-permute-start(bf16[1,512,384]{2,1,0:T(8,128)(2,1)S(1)} %get-tuple-element.79), channel_id=1, source_target_pairs={{0,1},{1,0},{2,3},{3,2},{4,5},{5,4},{6,7},{7,6},{8,9},{9,8},{10,11... | collective-permute-start | bytes 1179656 | tf_op jit(solution)/shard_map/ppermute | solution.py:181
  207.4 30.0 %collective-permute-start.1 = (bf16[1,512,384]{2,1,0:T(8,128)(2,1)S(1)}, bf16[1,512,384]{2,1,0:T(8,128)(2,1)S(1)}, u32[]{:S(2)}, u32[]{:S(2)}) collective-permute-start(bf16[1,512,384]{2,1,0:T(8,128)(2,1)S(1)} %get-tuple-element.80), channel_id=1, source_target_pairs={{0,2},{1,3},{2,0},{3,1},{4,6},{5,7},{6,4},{7,5},{8,10},{9,11},{10,... | collective-permute-start | bytes 1179656 | tf_op jit(solution)/shard_map/ppermute | solution.py:181
  209.0 28.4 %collective-permute-start.2 = (bf16[1,512,384]{2,1,0:T(8,128)(2,1)S(1)}, bf16[1,512,384]{2,1,0:T(8,128)(2,1)S(1)}, u32[]{:S(2)}, u32[]{:S(2)}) collective-permute-start(bf16[1,512,384]{2,1,0:T(8,128)(2,1)S(1)} %get-tuple-element.81), channel_id=1, source_target_pairs={{0,3},{1,2},{2,1},{3,0},{4,7},{5,6},{6,5},{7,4},{8,11},{9,10},{10,... | collective-permute-start | bytes 1179656 | tf_op jit(solution)/shard_map/ppermute | solution.py:181
  237.4 44.8 %copy-start = (bf16[1,512,384]{2,1,0:T(8,128)(2,1)}, bf16[1,512,384]{2,1,0:T(8,128)(2,1)S(1)}, u32[]{:S(2)}) copy-start(bf16[1,512,384]{2,1,0:T(8,128)(2,1)S(1)} %collective-permute-done) | copy-start | bytes 1179652
  237.4 44.8 %copy-start.2 = (bf16[1,512,384]{2,1,0:T(8,128)(2,1)}, bf16[1,512,384]{2,1,0:T(8,128)(2,1)S(1)}, u32[]{:S(2)}) copy-start(bf16[1,512,384]{2,1,0:T(8,128)(2,1)S(1)} %collective-permute-done.1) | copy-start | bytes 1179652
  237.5 44.8 %copy-start.4 = (bf16[1,512,384]{2,1,0:T(8,128)(2,1)}, bf16[1,512,384]{2,1,0:T(8,128)(2,1)S(1)}, u32[]{:S(2)}) copy-start(bf16[1,512,384]{2,1,0:T(8,128)(2,1)S(1)} %collective-permute-done.2) | copy-start | bytes 1179652
  237.5 41.4 %collective-permute-start.3 = (bf16[2,512,384]{2,1,0:T(8,128)(2,1)S(1)}, bf16[2,512,384]{2,1,0:T(8,128)(2,1)S(1)}, u32[]{:S(2)}, u32[]{:S(2)}) collective-permute-start(bf16[2,512,384]{2,1,0:T(8,128)(2,1)S(1)} %get-tuple-element.86), channel_id=1, source_target_pairs={{0,1},{1,0},{2,3},{3,2},{4,5},{5,4},{6,7},{7,6},{8,9},{9,8},{10,11... | collective-permute-start | bytes 2359304 | tf_op jit(solution)/shard_map/ppermute | solution.py:181
  245.6 36.6 %collective-permute-start.4 = (bf16[2,512,384]{2,1,0:T(8,128)(2,1)S(1)}, bf16[2,512,384]{2,1,0:T(8,128)(2,1)S(1)}, u32[]{:S(2)}, u32[]{:S(2)}) collective-permute-start(bf16[2,512,384]{2,1,0:T(8,128)(2,1)S(1)} %get-tuple-element.87), channel_id=1, source_target_pairs={{0,2},{1,3},{2,0},{3,1},{4,6},{5,7},{6,4},{7,5},{8,10},{9,11},{10,... | collective-permute-start | bytes 2359304 | tf_op jit(solution)/shard_map/ppermute | solution.py:181
  282.2 65.0 %all-to-all-start.3 = ((bf16[8,160,2048]{2,1,0:T(8,128)(2,1)}), bf16[8,160,2048]{2,1,0:T(8,128)(2,1)}, u32[]{:S(2)}, u32[]{:S(2)}) async-start(bf16[8,160,2048]{2,1,0:T(8,128)(2,1)} %bitcast.40), calls=%async_computation.4 | async-start | bytes 10485760 | tf_op jit(solution)/shard_map/all_to_all | solution.py:166
  286.9 97.8 %reduce-scatter.3.cloned.1.call-start = ((), (), s32[]{:S(2)}) async-start(), calls=%async_computation.7 | async-start | bytes 2621440 | tf_op jit(solution)/shard_map/reduce_scatter | solution.py:198
  293.8 118.0 %reduce-scatter.5.cloned.1.call-start = ((), (), s32[]{:S(2)}) async-start(), calls=%async_computation.9 | async-start | bytes 2621440 | tf_op jit(solution)/shard_map/reduce_scatter | solution.py:200
  293.8 34.7 %collective-permute-start.5 = (bf16[2,512,384]{2,1,0:T(8,128)(2,1)}, bf16[2,512,384]{2,1,0:T(8,128)(2,1)S(1)}, u32[]{:S(2)}, u32[]{:S(2)}) collective-permute-start(bf16[2,512,384]{2,1,0:T(8,128)(2,1)} %get-tuple-element.89), channel_id=1, source_target_pairs={{0,3},{1,2},{2,1},{3,0},{4,7},{5,6},{6,5},{7,4},{8,11},{9,10},{10,... | collective-permute-start | bytes 2359304 | tf_op jit(solution)/shard_map/ppermute | solution.py:181
  354.3 0.7 copy-start.7
  356.2 2.1 copy-start.1
  356.2 2.1 copy-start.3
  356.2 2.1 copy-start.5
  358.7 24.8 %collective-permute-start.6 = (bf16[3,512,384]{2,1,0:T(8,128)(2,1)S(1)}, bf16[3,512,384]{2,1,0:T(8,128)(2,1)S(1)}, u32[]{:S(2)}, u32[]{:S(2)}) collective-permute-start(bf16[3,512,384]{2,1,0:T(8,128)(2,1)S(1)} %fusion.3), channel_id=1, source_target_pairs={{0,16},{4,20},{8,24},{12,28},{16,0},{20,4},{24,8},{28,12},{1,17},{... | collective-permute-start | bytes 3538952 | tf_op jit(solution)/shard_map/ppermute | solution.py:204
Sparse Core Ops, SparseCore 0:
  9.6 48.7 all-gather.2
  71.6 45.0 all-gather.4
  293.9 65.3 reduce-scatter.2
  362.1 49.6 reduce-scatter.4
